TPU v7x, 512 devices: a whole 4x4x16 slice. The times are simulated.
512 devices in a mesh: dp: 32 (over z_lo, y), mp: 16 (over z_hi, x, core).
Axes of the slice: x: 4, y: 4, z: 16 (z_hi: 2, z_lo: 8; z = z_hi * 8 + z_lo), core: 2. Of those that a mesh axis runs over, the one named last changes fastest.
Arguments:
- hidden_in: bfloat16 [12288, 2048], P(('dp', 'mp')), may hold values from -12 to 12
- segment_ids: int32 [32, 384], P('dp'), may hold values from 0 to 7, never falling along the last dimension, each value on 1 to 192 neighbouring positions
- page_table: int32 [32, 3], P('dp'), may hold values from 0 to 2, each once within a row
- qkv_master: float32 [2048, 6144], P(('dp', 'mp')), may hold values from -0.3 to 0.3
- up_master: float32 [2048, 8192], P(('dp', 'mp')), may hold values from -0.125 to 0.125
- dense_weight: bfloat16 [2048, 2048], P('mp'), may hold values from -0.125 to 0.125
Outputs:
- hidden_out: bfloat16 [12288, 2048], P(('dp', 'mp'))
- activated: bfloat16 [12288, 8192], P('dp', 'mp')
- cache_pages: bfloat16 [96, 2, 16, 128, 128], P('dp', None, 'mp')
Inputs may be any that keep to these rules, and one draw needn't show every extreme that they name: `segment_ids`: within a group segment ids never fall; each request holds 1 to 192 tokens and one holds exactly that many. `page_table`: each row names every slot of its group once.
All inputs are finite; a program needn't handle non-finite values.
Results may differ from a plain program's by a relative error of at most 0.015.
Values may be sent and summed in bfloat16 or wider, within the bound.
A program may use at most 64 MiB of HBM per device.

v0:
```python
import jax
import jax.numpy as jnp
from jax import lax
from jax.sharding import PartitionSpec as P

H = 16
HD = 128
PAGE = 128


def layer_norm(values):
    mean_val = jnp.mean(values, -1, keepdims=True)
    centered = values - mean_val
    variance = jnp.mean(centered * centered, -1, keepdims=True)
    return centered * lax.rsqrt(variance + 1e-05)


def reorder_rows(weights, mp_count, dp_count):
    block = weights.shape[0] // (mp_count * dp_count)
    shaped = weights.reshape(mp_count, dp_count, block, weights.shape[1])
    return shaped.transpose(1, 0, 2, 3).reshape(weights.shape[0], weights.shape[1])


def attend(normed, qkv_w, segment, table, mp_index):
    group_rows = normed.shape[0]
    heads_dev = qkv_w.shape[1] // (3 * HD)
    joined = jnp.dot(normed, qkv_w, preferred_element_type=jnp.float32).astype(jnp.bfloat16)
    joined = joined.reshape(group_rows, heads_dev, 3, HD)
    query = joined[:, :, 0]
    keys = joined[:, :, 1]
    vals = joined[:, :, 2]
    head_ids = mp_index * heads_dev + jnp.arange(heads_dev)
    slopes = jnp.exp2(-8.0 * (head_ids + 1).astype(jnp.float32) / H)
    positions = jnp.arange(group_rows)
    distance = (positions[:, None] - positions[None, :]).astype(jnp.float32)
    allowed = (segment[:, None] == segment[None, :]) & (distance >= 0)
    scores = jnp.einsum("thd,shd->hts", query, keys, preferred_element_type=jnp.float32) / jnp.sqrt(
        jnp.float32(HD)
    )
    scores = scores - slopes[:, None, None] * distance[None]
    scores = jnp.where(allowed[None], scores, -jnp.inf)
    probs = jax.nn.softmax(scores, axis=-1).astype(jnp.bfloat16)
    context = jnp.einsum("hts,shd->thd", probs, vals, preferred_element_type=jnp.float32).astype(
        jnp.bfloat16
    )
    context = context.reshape(group_rows, heads_dev * HD)
    key_vals = jnp.stack([keys, vals], 1)
    pages_here = group_rows // PAGE
    key_vals = key_vals.reshape(pages_here, PAGE, 2, heads_dev, HD).transpose(0, 2, 3, 1, 4)
    cache = jnp.zeros((pages_here, 2, heads_dev, PAGE, HD), jnp.bfloat16).at[table].set(key_vals)
    return (context, cache)


def local(hidden_in, segment_ids, page_table, qkv_master, up_master, dense_weight):
    mp_count = lax.axis_size("mp")
    dp_count = lax.axis_size("dp")
    mp_index = lax.axis_index("mp")
    qkv_bf = qkv_master.astype(jnp.bfloat16)
    up_bf = up_master.astype(jnp.bfloat16)
    qkv_rows, up_rows = (
        lax.all_gather(qkv_bf, "dp", axis=0, tiled=True),
        lax.all_gather(up_bf, "dp", axis=0, tiled=True),
    )
    qkv_cols, up_cols = (
        lax.all_to_all(qkv_rows, "mp", split_axis=1, concat_axis=0, tiled=True),
        lax.all_to_all(up_rows, "mp", split_axis=1, concat_axis=0, tiled=True),
    )
    qkv_w = reorder_rows(qkv_cols, mp_count, dp_count)
    up_w = reorder_rows(up_cols, mp_count, dp_count)
    normed_own = layer_norm(hidden_in.astype(jnp.float32)).astype(jnp.bfloat16)
    normed = lax.all_gather(normed_own, "mp", axis=0, tiled=True)
    context, cache = attend(normed, qkv_w, segment_ids[0], page_table[0], mp_index)
    share = lax.psum_scatter(
        jnp.dot(context, dense_weight, preferred_element_type=jnp.float32).astype(jnp.bfloat16),
        "mp",
        scatter_dimension=0,
        tiled=True,
    ).astype(jnp.float32)
    stream_own = hidden_in.astype(jnp.float32) + share
    normed_two = lax.all_gather(
        layer_norm(stream_own).astype(jnp.bfloat16), "mp", axis=0, tiled=True
    )
    upper = jnp.dot(normed_two, up_w, preferred_element_type=jnp.float32)
    activated = jax.nn.gelu(upper, approximate=True).astype(jnp.bfloat16)
    return (stream_own.astype(jnp.bfloat16), activated, cache)


def solution(mesh):
    placed = (
        P(("dp", "mp"), None),
        P("dp", None),
        P("dp", None),
        P(("dp", "mp"), None),
        P(("dp", "mp"), None),
        P("mp", None),
    )
    return jax.shard_map(
        local,
        mesh=mesh,
        in_specs=placed,
        out_specs=(P(("dp", "mp"), None), P("dp", "mp"), P("dp", None, "mp", None, None)),
        check_vma=False,
    )
```

profile of v0, /device:TPU:1, one launch (start us, length us, event | category | flops | bytes accessed | tf_op | source)
XLA Modules:
  0.0 827.7 jit_solution(535030976519693917)
XLA Ops:
  7.2 1.6 convert_bitcast_fusion.1
  8.9 1.6 convert_bitcast_fusion
  10.5 207.6 %all-gather.11.cloned.1.call-done = bf16[32,4,6144]{2,1,0:T(4,128)(2,1)} async-done(((bf16[1,4,6144]{2,1,0:T(4,128)(2,1)}), bf16[32,4,6144]{2,1,0:T(4,128)(2,1)}) %all-gather.11.cloned.1.call-update) | async-done | bytes 1572880 | tf_op jit(solution)/shard_map/all_gather | solution.py:61
  218.1 3.1 all_to_all.24
  221.1 1.6 copy.20
  222.7 54.5 %all-to-all-start = ((bf16[128,16,384]{2,0,1:T(8,128)(2,1)}), bf16[128,16,384]{2,0,1:T(8,128)(2,1)}, u32[]{:S(2)}, u32[]{:S(2)}) async-start(bf16[128,16,384]{2,0,1:T(8,128)(2,1)} %copy.20), calls=%async_computation | async-start | bytes 3145728 | tf_op jit(solution)/shard_map/all_to_all | solution.py:65
  277.3 0.1 convert_reduce_fusion
  277.4 0.2 fusion.19
  277.7 0.7 fusion.20
  278.4 184.5 %all-gather.13.cloned.1.call-done = bf16[32,4,8192]{2,1,0:T(4,128)(2,1)} async-done(((bf16[1,4,8192]{2,1,0:T(4,128)(2,1)}), bf16[32,4,8192]{2,1,0:T(4,128)(2,1)}) %all-gather.13.cloned.1.call-update) | async-done | bytes 2097168 | tf_op jit(solution)/shard_map/all_gather | solution.py:62
  463.0 3.3 all_to_all.27
  466.2 2.5 copy.25
  468.7 54.6 %all-to-all-start.1 = ((bf16[128,16,512]{2,0,1:T(8,128)(2,1)}), bf16[128,16,512]{2,0,1:T(8,128)(2,1)S(1)}, u32[]{:S(2)}, u32[]{:S(2)}) async-start(bf16[128,16,512]{2,0,1:T(8,128)(2,1)} %copy.25), calls=%async_computation.2 | async-start | bytes 4194304 | tf_op jit(solution)/shard_map/all_to_all | solution.py:66
  523.5 2.3 copy.21
  525.8 2.0 copy.22
  527.8 3.7 reshape.134
  531.6 93.0 %all-gather.7.cloned.1.call-done = bf16[384,2048]{1,0:T(8,128)(2,1)} async-done(((bf16[24,2048]{1,0:T(8,128)(2,1)}), bf16[384,2048]{1,0:T(8,128)(2,1)}) %all-gather.7.cloned.1.call-update) | async-done | bytes 1572880 | tf_op jit(solution)/shard_map/all_gather | solution.py:71
  624.6 2.9 convolution_convert_fusion.1
  627.5 0.7 copy-done.3
  628.2 0.4 fusion.31
  628.8 2.8 convolution_convert_fusion
  631.6 0.2 all-gather.9.cloned.1.call-start
  631.9 103.5 %reduce-scatter.2.cloned.1.call-done = bf16[24,2048]{1,0:T(8,128)(2,1)} async-done(((bf16[384,2048]{1,0:T(8,128)(2,1)}), bf16[24,2048]{1,0:T(8,128)(2,1)}) %reduce-scatter.2.cloned.1.call-update) | async-done | bytes 98320 | tf_op jit(solution)/shard_map/reduce_scatter | solution.py:73
  735.4 1.0 fusion.21
  736.4 1.1 multiply_reduce_fusion
  737.5 1.6 multiply_convert_fusion
  739.6 0.8 scatter_fusion
  740.4 1.2 copy.26
  741.6 2.0 copy.27
  743.6 2.1 reshape.141
  745.6 71.5 %all-gather.9.cloned.1.call-done = bf16[384,2048]{1,0:T(8,128)(2,1)} async-done(((bf16[24,2048]{1,0:T(8,128)(2,1)}), bf16[384,2048]{1,0:T(8,128)(2,1)}) %all-gather.9.cloned.1.call-update) | async-done | bytes 1572880 | tf_op jit(solution)/shard_map/all_gather | solution.py:80
  817.2 3.9 fusion.10
  (37 shorter events, 0.8 us)
Async XLA Ops:
  7.2 621.6 %copy-start = (bf16[128,2048]{1,0:T(8,128)(2,1)S(1)}, bf16[128,2048]{1,0:T(8,128)(2,1)}, u32[]{:S(2)}) copy-start(bf16[128,2048]{1,0:T(8,128)(2,1)} %param.11) | copy-start | bytes 1572868
  7.2 210.9 %all-gather.11.cloned.1.call-start = ((), (), s32[]{:S(2)}) async-start(), calls=%async_computation.6 | async-start | bytes 1622016 | tf_op jit(solution)/shard_map/all_gather | solution.py:61
  8.8 454.1 %all-gather.13.cloned.1.call-start = ((), (), s32[]{:S(2)}) async-start(), calls=%async_computation.7 | async-start | bytes 2162688 | tf_op jit(solution)/shard_map/all_gather | solution.py:62
  222.7 54.6 %copy-start.1 = (bf16[24,2048]{1,0:T(8,128)(2,1)S(1)}, bf16[24,2048]{1,0:T(8,128)(2,1)}, u32[]{:S(2)}) copy-start(bf16[24,2048]{1,0:T(8,128)(2,1)} %param.6) | copy-start | bytes 294916
  222.7 246.0 %all-to-all-start = ((bf16[128,16,384]{2,0,1:T(8,128)(2,1)}), bf16[128,16,384]{2,0,1:T(8,128)(2,1)}, u32[]{:S(2)}, u32[]{:S(2)}) async-start(bf16[128,16,384]{2,0,1:T(8,128)(2,1)} %copy.20), calls=%async_computation | async-start | bytes 3145728 | tf_op jit(solution)/shard_map/all_to_all | solution.py:65
  277.2 347.4 %all-gather.7.cloned.1.call-start = ((), (), s32[]{:S(2)}) async-start(), calls=%async_computation.3 | async-start | bytes 1671168 | tf_op jit(solution)/shard_map/all_gather | solution.py:71
  468.7 54.7 %copy-start.5 = (s32[1,384]{1,0:T(1,128)S(1)}, s32[1,384]{1,0:T(1,128)}, u32[]{:S(2)}) copy-start(s32[1,384]{1,0:T(1,128)} %param.7) | copy-start | bytes 4612
  468.7 271.7 %all-to-all-start.1 = ((bf16[128,16,512]{2,0,1:T(8,128)(2,1)}), bf16[128,16,512]{2,0,1:T(8,128)(2,1)S(1)}, u32[]{:S(2)}, u32[]{:S(2)}) async-start(bf16[128,16,512]{2,0,1:T(8,128)(2,1)} %copy.25), calls=%async_computation.2 | async-start | bytes 4194304 | tf_op jit(solution)/shard_map/all_to_all | solution.py:66
  523.4 212.0 %reduce-scatter.2.cloned.1.call-start = ((), (), s32[]{:S(2)}) async-start(), calls=%async_computation.4 | async-start | bytes 1671168 | tf_op jit(solution)/shard_map/reduce_scatter | solution.py:73
  627.5 0.7 copy-start.3
  631.6 107.5 %copy-start.6 = (s32[1,3]{1,0:T(1,128)S(1)}, s32[1,3]{1,0:T(1,128)}, u32[]{:S(2)}) copy-start(s32[1,3]{1,0:T(1,128)} %param.8) | copy-start | bytes 40
  631.6 107.6 %copy-start.4 = (bf16[384,384]{0,1:T(8,128)(2,1)S(1)}, bf16[384,384]{0,1:T(8,128)(2,1)}, u32[]{:S(2)}) copy-start(bf16[384,384]{0,1:T(8,128)(2,1)} %copy-done.3) | copy-start | bytes 884740
  631.6 185.6 %all-gather.9.cloned.1.call-start = ((), (), s32[]{:S(2)}) async-start(), calls=%async_computation.5 | async-start | bytes 1671168 | tf_op jit(solution)/shard_map/all_gather | solution.py:80
  740.4 1.2 copy-start.2
Sparse Core Ops, SparseCore 0:
  10.7 207.3 all-gather.10
  220.7 242.2 all-gather.12
  466.9 157.6 all-gather.6
  631.8 103.5 reduce-scatter.1
  739.3 77.8 all-gather.8
where the time goes:
time: 828 us
  waiting for transfers between devices  660 us (80%)
  starting transfers between devices  110 us (13%)
  local copies, waits for them, and re-layouts  25.5 us (3%)
  between operations  14 us (2%)
  matrix products  10.1 us (1%)
    all_gather x1, waiting for transfers between devices, local(): lax.all_gather(qkv_bf, 'dp', axis=0, tiled=True)  208 us
    all_gather x1, waiting for transfers between devices, local(): lax.all_gather(up_bf, 'dp', axis=0, tiled=True)  185 us
    reduce_scatter x1, waiting for transfers between devices, local(): lax.psum_scatter(jnp.dot(context, dense_weight, preferred_element_type=jn...  104 us
    all_gather x1, waiting for transfers between devices, local(): normed = lax.all_gather(normed_own, 'mp', axis=0, tiled=True)  93 us
    all_gather x1, waiting for transfers between devices, local(): lax.all_gather(layer_norm(stream_own).astype(jnp.bfloat16), 'mp', axis=0,...  71.5 us
    all_to_all x1, starting transfers between devices, local(): lax.all_to_all(up_rows, 'mp', split_axis=1, concat_axis=0, tiled=True)  54.6 us
    all_to_all x1, starting transfers between devices, local(): lax.all_to_all(qkv_rows, 'mp', split_axis=1, concat_axis=0, tiled=True)  54.5 us
  transfers between devices with their start and end apart: 7, of which 5 were waited for; matrix products, arithmetic and copies ran while one was open for 4% of the time, Pallas kernels for 0%

commit v1 on v0

--- a/solution.py
+++ b/solution.py
@@ -15,10 +15,10 @@
     return centered * lax.rsqrt(variance + 1e-05)
 
 
-def reorder_rows(weights, mp_count, dp_count):
-    block = weights.shape[0] // (mp_count * dp_count)
-    shaped = weights.reshape(mp_count, dp_count, block, weights.shape[1])
-    return shaped.transpose(1, 0, 2, 3).reshape(weights.shape[0], weights.shape[1])
+def gather_rows(x, axis):
+    n = lax.axis_size(axis)
+    tiled = jnp.concatenate([x] * n, axis=0)
+    return lax.all_to_all(tiled, axis, split_axis=0, concat_axis=0, tiled=True)
 
 
 def attend(normed, qkv_w, segment, table, mp_index):
@@ -53,33 +53,24 @@
 
 def local(hidden_in, segment_ids, page_table, qkv_master, up_master, dense_weight):
     mp_count = lax.axis_size("mp")
-    dp_count = lax.axis_size("dp")
     mp_index = lax.axis_index("mp")
     qkv_bf = qkv_master.astype(jnp.bfloat16)
     up_bf = up_master.astype(jnp.bfloat16)
-    qkv_rows, up_rows = (
-        lax.all_gather(qkv_bf, "dp", axis=0, tiled=True),
-        lax.all_gather(up_bf, "dp", axis=0, tiled=True),
+    qkv_w = gather_rows(
+        lax.all_to_all(qkv_bf, "mp", split_axis=1, concat_axis=0, tiled=True), "dp"
     )
-    qkv_cols, up_cols = (
-        lax.all_to_all(qkv_rows, "mp", split_axis=1, concat_axis=0, tiled=True),
-        lax.all_to_all(up_rows, "mp", split_axis=1, concat_axis=0, tiled=True),
+    up_w = gather_rows(
+        lax.all_to_all(up_bf, "mp", split_axis=1, concat_axis=0, tiled=True), "dp"
     )
-    qkv_w = reorder_rows(qkv_cols, mp_count, dp_count)
-    up_w = reorder_rows(up_cols, mp_count, dp_count)
     normed_own = layer_norm(hidden_in.astype(jnp.float32)).astype(jnp.bfloat16)
-    normed = lax.all_gather(normed_own, "mp", axis=0, tiled=True)
+    normed = gather_rows(normed_own, "mp")
     context, cache = attend(normed, qkv_w, segment_ids[0], page_table[0], mp_index)
-    share = lax.psum_scatter(
-        jnp.dot(context, dense_weight, preferred_element_type=jnp.float32).astype(jnp.bfloat16),
-        "mp",
-        scatter_dimension=0,
-        tiled=True,
-    ).astype(jnp.float32)
+    partial = jnp.dot(context, dense_weight, preferred_element_type=jnp.float32).astype(jnp.bfloat16)
+    parts = lax.all_to_all(partial, "mp", split_axis=0, concat_axis=0, tiled=True)
+    rows = hidden_in.shape[0]
+    share = jnp.sum(parts.reshape(mp_count, rows, -1).astype(jnp.float32), axis=0)
     stream_own = hidden_in.astype(jnp.float32) + share
-    normed_two = lax.all_gather(
-        layer_norm(stream_own).astype(jnp.bfloat16), "mp", axis=0, tiled=True
-    )
+    normed_two = gather_rows(layer_norm(stream_own).astype(jnp.bfloat16), "mp")
     upper = jnp.dot(normed_two, up_w, preferred_element_type=jnp.float32)
     activated = jax.nn.gelu(upper, approximate=True).astype(jnp.bfloat16)
     return (stream_own.astype(jnp.bfloat16), activated, cache)

time: 828 us -> 510 us (0.62)
  the two profiles are of different devices: /device:TPU:1 before, /device:TPU:33 now
where the time goes in v1:
time: 510 us; the launch traced here: 509 us
  waiting for transfers between devices  355 us (70%)
  starting transfers between devices  71.7 us (14%)
  local copies, waits for them, and re-layouts  50.5 us (10%)
  other arithmetic  23.4 us (5%)
  matrix products  8.25 us (2%)
    all_to_all x4, waiting for transfers between devices, gather_rows(): return lax.all_to_all(tiled, axis, split_axis=0, concat_axis=0, tiled=True)  284 us
    all_to_all x1, waiting for transfers between devices, local(): lax.all_to_all(partial, 'mp', split_axis=0, concat_axis=0, tiled=True)  60.8 us
    unnamed x90, local copies, waits for them, and re-layouts  47.7 us
    all_to_all x4, starting transfers between devices, gather_rows(): return lax.all_to_all(tiled, axis, split_axis=0, concat_axis=0, tiled=True)  38.3 us
    all_to_all x1, starting transfers between devices, local(): lax.all_to_all(qkv_bf, 'mp', split_axis=1, concat_axis=0, tiled=True)  17.3 us
    unnamed x17, other arithmetic  16.9 us
    all_to_all x1, starting transfers between devices, local(): lax.all_to_all(up_bf, 'mp', split_axis=1, concat_axis=0, tiled=True)  11.3 us
  transfers between devices with their start and end apart: 7, of which 6 were waited for; matrix products, arithmetic and copies ran while one was open for 15% of the time, Pallas kernels for 0%

profile of v1, /device:TPU:33, one launch (start us, length us, event | category | flops | bytes accessed | tf_op | source)
XLA Modules:
  0.0 509.2 jit_solution(15863179200196846109)
XLA Ops:
  0.7 1.6 convert_element_type.55
  2.3 17.3 %all-to-all-start.1 = ((bf16[4,16,384]{2,0,1:T(4,128)(2,1)}), bf16[4,16,384]{2,0,1:T(4,128)(2,1)S(1)}, u32[]{:S(2)}, u32[]{:S(2)}) async-start(bf16[4,16,384]{2,0,1:T(4,128)(2,1)} %bitcast.2), calls=%async_computation.1 | async-start | bytes 98304 | tf_op jit(solution)/shard_map/all_to_all | solution.py:60
  19.6 1.0 convert_reduce_fusion.1
  20.6 1.1 fusion.19
  21.7 1.6 constant_dynamic-update-slice_fusion.15
  23.4 1.6 constant_dynamic-update-slice_fusion.14
  25.0 1.6 constant_dynamic-update-slice_fusion.13
  26.6 1.6 constant_dynamic-update-slice_fusion.12
  28.2 1.6 constant_dynamic-update-slice_fusion.11
  29.8 1.6 constant_dynamic-update-slice_fusion.10
  31.4 0.7 constant_dynamic-update-slice_fusion.9
  34.3 0.7 constant_dynamic-update-slice_fusion.5
  37.2 0.7 constant_dynamic-update-slice_fusion.1
  37.9 0.7 constant_dynamic-update-slice_fusion
  38.6 14.4 %all-to-all-start = ((bf16[16,24,2048]{2,1,0:T(8,128)(2,1)}), bf16[16,24,2048]{2,1,0:T(8,128)(2,1)S(1)}, u32[]{:S(2)}, u32[]{:S(2)}) async-start(bf16[16,24,2048]{2,1,0:T(8,128)(2,1)} %bitcast), calls=%async_computation | async-start | bytes 3145728 | tf_op jit(solution)/shard_map/all_to_all | solution.py:21
  72.9 60.7 %all-to-all-done = bf16[16,24,2048]{2,1,0:T(8,128)(2,1)S(1)} async-done(((bf16[16,24,2048]{2,1,0:T(8,128)(2,1)}), bf16[16,24,2048]{2,1,0:T(8,128)(2,1)S(1)}, u32[]{:S(2)}, u32[]{:S(2)}) %all-to-all-start) | async-done | bytes 1572896 | tf_op jit(solution)/shard_map/all_to_all | solution.py:21
  133.6 8.0 %all-to-all-start.2 = ((bf16[32,64,384]{2,1,0:T(8,128)(2,1)}), bf16[32,64,384]{2,1,0:T(8,128)(2,1)}, u32[]{:S(2)}, u32[]{:S(2)}) async-start(bf16[32,64,384]{2,1,0:T(8,128)(2,1)} %bitcast.4), calls=%async_computation.2 | async-start | bytes 3145728 | tf_op jit(solution)/shard_map/all_to_all | solution.py:21
  142.4 67.1 %all-to-all-done.2 = bf16[32,64,384]{2,1,0:T(8,128)(2,1)} async-done(((bf16[32,64,384]{2,1,0:T(8,128)(2,1)}), bf16[32,64,384]{2,1,0:T(8,128)(2,1)}, u32[]{:S(2)}, u32[]{:S(2)}) %all-to-all-start.2) | async-done | bytes 1572896 | tf_op jit(solution)/shard_map/all_to_all | solution.py:21
  209.5 11.3 %all-to-all-start.5 = ((bf16[4,16,512]{2,0,1:T(4,128)(2,1)}), bf16[4,16,512]{2,0,1:T(4,128)(2,1)S(1)}, u32[]{:S(2)}, u32[]{:S(2)}) async-start(bf16[4,16,512]{2,0,1:T(4,128)(2,1)} %bitcast.16), calls=%async_computation.5 | async-start | bytes 131072 | tf_op jit(solution)/shard_map/all_to_all | solution.py:63
  220.8 2.4 convolution_convert_fusion.1
  223.7 2.0 convolution_convert_fusion
  225.7 9.7 %all-to-all-done.5 = bf16[4,16,512]{2,0,1:T(4,128)(2,1)S(1)} async-done(((bf16[4,16,512]{2,0,1:T(4,128)(2,1)}), bf16[4,16,512]{2,0,1:T(4,128)(2,1)S(1)}, u32[]{:S(2)}, u32[]{:S(2)}) %all-to-all-start.5) | async-done | bytes 65568 | tf_op jit(solution)/shard_map/all_to_all | solution.py:63
  235.4 4.7 all-to-all-start.3
  260.1 60.8 %all-to-all-done.3 = bf16[16,24,2048]{2,1,0:T(8,128)(2,1)S(1)} async-done(((bf16[16,24,2048]{2,1,0:T(8,128)(2,1)}), bf16[16,24,2048]{2,1,0:T(8,128)(2,1)S(1)}, u32[]{:S(2)}, u32[]{:S(2)}) %all-to-all-start.3) | async-done | bytes 1572896 | tf_op jit(solution)/shard_map/all_to_all | solution.py:69
  320.9 4.5 all-to-all-start.6
  325.9 0.8 multiply_reduce_fusion
  326.7 0.7 constant_dynamic-update-slice_fusion.63
  337.0 76.5 %all-to-all-done.6 = bf16[32,64,512]{2,1,0:T(8,128)(2,1)} async-done(((bf16[32,64,512]{2,1,0:T(8,128)(2,1)}), bf16[32,64,512]{2,1,0:T(8,128)(2,1)}, u32[]{:S(2)}, u32[]{:S(2)}) %all-to-all-start.6) | async-done | bytes 2097184 | tf_op jit(solution)/shard_map/all_to_all | solution.py:21
  413.5 11.3 %all-to-all-start.4 = ((bf16[16,24,2048]{2,1,0:T(8,128)(2,1)}), bf16[16,24,2048]{2,1,0:T(8,128)(2,1)S(1)}, u32[]{:S(2)}, u32[]{:S(2)}) async-start(bf16[16,24,2048]{2,1,0:T(8,128)(2,1)} %bitcast.14), calls=%async_computation.4 | async-start | bytes 3145728 | tf_op jit(solution)/shard_map/all_to_all | solution.py:21
  425.3 0.8 scatter_fusion
  426.1 79.7 %all-to-all-done.4 = bf16[16,24,2048]{2,1,0:T(8,128)(2,1)S(1)} async-done(((bf16[16,24,2048]{2,1,0:T(8,128)(2,1)}), bf16[16,24,2048]{2,1,0:T(8,128)(2,1)S(1)}, u32[]{:S(2)}, u32[]{:S(2)}) %all-to-all-start.4) | async-done | bytes 1572896 | tf_op jit(solution)/shard_map/all_to_all | solution.py:21
  505.8 3.5 fusion.10
  (117 shorter events, 55.7 us)
Async XLA Ops:
  0.6 223.1 %copy-start = (bf16[128,2048]{1,0:T(8,128)(2,1)S(1)}, bf16[128,2048]{1,0:T(8,128)(2,1)}, u32[]{:S(2)}) copy-start(bf16[128,2048]{1,0:T(8,128)(2,1)} %param.11) | copy-start | bytes 1572868
  0.6 30.8 %copy-start.1 = (bf16[24,2048]{1,0:T(8,128)(2,1)S(1)}, bf16[24,2048]{1,0:T(8,128)(2,1)}, u32[]{:S(2)}) copy-start(bf16[24,2048]{1,0:T(8,128)(2,1)} %param.6) | copy-start | bytes 294916
  2.3 36.4 %all-to-all-start.1 = ((bf16[4,16,384]{2,0,1:T(4,128)(2,1)}), bf16[4,16,384]{2,0,1:T(4,128)(2,1)S(1)}, u32[]{:S(2)}, u32[]{:S(2)}) async-start(bf16[4,16,384]{2,0,1:T(4,128)(2,1)} %bitcast.2), calls=%async_computation.1 | async-start | bytes 98304 | tf_op jit(solution)/shard_map/all_to_all | solution.py:60
  38.6 95.0 %all-to-all-start = ((bf16[16,24,2048]{2,1,0:T(8,128)(2,1)}), bf16[16,24,2048]{2,1,0:T(8,128)(2,1)S(1)}, u32[]{:S(2)}, u32[]{:S(2)}) async-start(bf16[16,24,2048]{2,1,0:T(8,128)(2,1)} %bitcast), calls=%async_computation | async-start | bytes 3145728 | tf_op jit(solution)/shard_map/all_to_all | solution.py:21
  133.6 8.1 %copy-start.3 = (f32[4,8192]{1,0:T(4,128)S(1)}, f32[4,8192]{1,0:T(4,128)}, u32[]{:S(2)}) copy-start(f32[4,8192]{1,0:T(4,128)} %param.10) | copy-start | bytes 393220
  133.6 8.8 %copy-start.4 = (s32[1,384]{1,0:T(1,128)S(1)}, s32[1,384]{1,0:T(1,128)}, u32[]{:S(2)}) copy-start(s32[1,384]{1,0:T(1,128)} %param.7) | copy-start | bytes 4612
  133.6 75.9 %all-to-all-start.2 = ((bf16[32,64,384]{2,1,0:T(8,128)(2,1)}), bf16[32,64,384]{2,1,0:T(8,128)(2,1)}, u32[]{:S(2)}, u32[]{:S(2)}) async-start(bf16[32,64,384]{2,1,0:T(8,128)(2,1)} %bitcast.4), calls=%async_computation.2 | async-start | bytes 3145728 | tf_op jit(solution)/shard_map/all_to_all | solution.py:21
  209.5 25.9 %all-to-all-start.5 = ((bf16[4,16,512]{2,0,1:T(4,128)(2,1)}), bf16[4,16,512]{2,0,1:T(4,128)(2,1)S(1)}, u32[]{:S(2)}, u32[]{:S(2)}) async-start(bf16[4,16,512]{2,0,1:T(4,128)(2,1)} %bitcast.16), calls=%async_computation.5 | async-start | bytes 131072 | tf_op jit(solution)/shard_map/all_to_all | solution.py:63
  235.4 85.5 %all-to-all-start.3 = ((bf16[16,24,2048]{2,1,0:T(8,128)(2,1)}), bf16[16,24,2048]{2,1,0:T(8,128)(2,1)S(1)}, u32[]{:S(2)}, u32[]{:S(2)}) async-start(bf16[16,24,2048]{2,1,0:T(8,128)(2,1)} %bitcast.57), calls=%async_computation.3 | async-start | bytes 3145728 | tf_op jit(solution)/shard_map/all_to_all | solution.py:69
  320.9 92.6 %all-to-all-start.6 = ((bf16[32,64,512]{2,1,0:T(8,128)(2,1)}), bf16[32,64,512]{2,1,0:T(8,128)(2,1)}, u32[]{:S(2)}, u32[]{:S(2)}) async-start(bf16[32,64,512]{2,1,0:T(8,128)(2,1)} %bitcast.18), calls=%async_computation.6 | async-start | bytes 4194304 | tf_op jit(solution)/shard_map/all_to_all | solution.py:21
  413.5 11.3 %copy-start.5 = (s32[1,3]{1,0:T(1,128)S(1)}, s32[1,3]{1,0:T(1,128)}, u32[]{:S(2)}) copy-start(s32[1,3]{1,0:T(1,128)} %param.8) | copy-start | bytes 40
  413.5 92.2 %all-to-all-start.4 = ((bf16[16,24,2048]{2,1,0:T(8,128)(2,1)}), bf16[16,24,2048]{2,1,0:T(8,128)(2,1)S(1)}, u32[]{:S(2)}, u32[]{:S(2)}) async-start(bf16[16,24,2048]{2,1,0:T(8,128)(2,1)} %bitcast.14), calls=%async_computation.4 | async-start | bytes 3145728 | tf_op jit(solution)/shard_map/all_to_all | solution.py:21
  426.1 83.1 %copy-start.2 = (bf16[3,2,128,128]{3,2,1,0:T(8,128)(2,1)}, bf16[3,2,128,128]{3,2,1,0:T(8,128)(2,1)S(1)}, u32[]{:S(2)}) copy-start(bf16[3,2,128,128]{3,2,1,0:T(8,128)(2,1)S(1)} %scatter_fusion) | copy-start | bytes 589828

commit v2 on v1

--- a/solution.py
+++ b/solution.py
@@ -1,11 +1,16 @@
+import functools
+
 import jax
 import jax.numpy as jnp
 from jax import lax
+from jax.experimental import pallas as pl
+from jax.experimental.pallas import tpu as pltpu
 from jax.sharding import PartitionSpec as P
 
 H = 16
 HD = 128
 PAGE = 128
+MESH = pl.DeviceIdType.MESH
 
 
 def layer_norm(values):
@@ -15,10 +20,54 @@
     return centered * lax.rsqrt(variance + 1e-05)
 
 
-def gather_rows(x, axis):
+def exchange_kernel(n, axis, spread, count, *refs):
+    ins, outs = refs[:count], refs[count:2 * count]
+    send_sem, recv_sem = refs[2 * count], refs[2 * count + 1]
+    me = lax.axis_index(axis)
+    barrier = pltpu.get_barrier_semaphore()
+    for step in range(1, n):
+        peer = lax.rem(me + step, n)
+        pl.semaphore_signal(barrier, inc=1, device_id={axis: peer}, device_id_type=MESH)
+    pl.semaphore_wait(barrier, n - 1)
+    copies = []
+    for a in range(count):
+        for step in range(1, n):
+            peer = lax.rem(me + step, n)
+            src = ins[a].at[peer] if spread else ins[a]
+            slot = a * (n - 1) + step - 1
+            copy = pltpu.make_async_remote_copy(
+                src_ref=src,
+                dst_ref=outs[a].at[me],
+                send_sem=send_sem.at[slot],
+                recv_sem=recv_sem.at[slot],
+                device_id={axis: peer},
+                device_id_type=MESH,
+            )
+            copy.start()
+            copies.append(copy)
+    for a in range(count):
+        outs[a][me] = ins[a][me] if spread else ins[a][...]
+    for copy in copies:
+        copy.wait()
+
+
+def exchange(xs, axis, spread, cid):
     n = lax.axis_size(axis)
-    tiled = jnp.concatenate([x] * n, axis=0)
-    return lax.all_to_all(tiled, axis, split_axis=0, concat_axis=0, tiled=True)
+    count = len(xs)
+    outs = [
+        jax.ShapeDtypeStruct((n,) + (x.shape[1:] if spread else x.shape), x.dtype) for x in xs
+    ]
+    return pl.pallas_call(
+        functools.partial(exchange_kernel, n, axis, spread, count),
+        out_shape=outs,
+        in_specs=[pl.BlockSpec(memory_space=pltpu.VMEM)] * count,
+        out_specs=[pl.BlockSpec(memory_space=pltpu.VMEM)] * count,
+        scratch_shapes=[
+            pltpu.SemaphoreType.DMA((count * (n - 1),)),
+            pltpu.SemaphoreType.DMA((count * (n - 1),)),
+        ],
+        compiler_params=pltpu.CompilerParams(collective_id=cid, has_side_effects=True),
+    )(*xs)
 
 
 def attend(normed, qkv_w, segment, table, mp_index):
@@ -54,23 +103,28 @@
 def local(hidden_in, segment_ids, page_table, qkv_master, up_master, dense_weight):
     mp_count = lax.axis_size("mp")
     mp_index = lax.axis_index("mp")
-    qkv_bf = qkv_master.astype(jnp.bfloat16)
-    up_bf = up_master.astype(jnp.bfloat16)
-    qkv_w = gather_rows(
-        lax.all_to_all(qkv_bf, "mp", split_axis=1, concat_axis=0, tiled=True), "dp"
+    rows_w = qkv_master.shape[0]
+    qkv_t = qkv_master.astype(jnp.bfloat16).reshape(rows_w, mp_count, -1).transpose(1, 0, 2)
+    up_t = up_master.astype(jnp.bfloat16).reshape(rows_w, mp_count, -1).transpose(1, 0, 2)
+    qkv_blk, up_blk = exchange([qkv_t, up_t], "mp", True, 0)
+    qkv_g, up_g = exchange(
+        [qkv_blk.reshape(mp_count * rows_w, -1), up_blk.reshape(mp_count * rows_w, -1)],
+        "dp",
+        False,
+        1,
     )
-    up_w = gather_rows(
-        lax.all_to_all(up_bf, "mp", split_axis=1, concat_axis=0, tiled=True), "dp"
-    )
+    qkv_w = qkv_g.reshape(-1, qkv_g.shape[-1])
+    up_w = up_g.reshape(-1, up_g.shape[-1])
+    rows = hidden_in.shape[0]
     normed_own = layer_norm(hidden_in.astype(jnp.float32)).astype(jnp.bfloat16)
-    normed = gather_rows(normed_own, "mp")
+    normed = exchange([normed_own], "mp", False, 2)[0].reshape(mp_count * rows, -1)
     context, cache = attend(normed, qkv_w, segment_ids[0], page_table[0], mp_index)
     partial = jnp.dot(context, dense_weight, preferred_element_type=jnp.float32).astype(jnp.bfloat16)
-    parts = lax.all_to_all(partial, "mp", split_axis=0, concat_axis=0, tiled=True)
-    rows = hidden_in.shape[0]
-    share = jnp.sum(parts.reshape(mp_count, rows, -1).astype(jnp.float32), axis=0)
+    parts = exchange([partial.reshape(mp_count, rows, -1)], "mp", True, 3)[0]
+    share = jnp.sum(parts.astype(jnp.float32), axis=0)
     stream_own = hidden_in.astype(jnp.float32) + share
-    normed_two = gather_rows(layer_norm(stream_own).astype(jnp.bfloat16), "mp")
+    normed_two = exchange([layer_norm(stream_own).astype(jnp.bfloat16)], "mp", False, 4)[0]
+    normed_two = normed_two.reshape(mp_count * rows, -1)
     upper = jnp.dot(normed_two, up_w, preferred_element_type=jnp.float32)
     activated = jax.nn.gelu(upper, approximate=True).astype(jnp.bfloat16)
     return (stream_own.astype(jnp.bfloat16), activated, cache)

time: 510 us -> 497 us (0.975)
  the two profiles are of different devices: /device:TPU:33 before, /device:TPU:239 now
where the time goes in v2:
time: 497 us; the launch traced here: 496 us
  Pallas kernels  472 us (95%)
  other arithmetic  10 us (2%)
  matrix products  8.09 us (2%)
  local copies, waits for them, and re-layouts  5.08 us (1%)
    pallas_call x5, Pallas kernels, exchange(): pl.pallas_call(functools.partial(exchange_kernel, n, axis, spread, count)...  472 us

profile of v2, /device:TPU:239, one launch (start us, length us, event | category | flops | bytes accessed | tf_op | source)
XLA Modules:
  0.0 495.8 jit_solution(7401228677245370539)
XLA Ops:
  0.6 0.0 copy-start
  0.6 1.6 convert_element_type.56
  2.3 1.5 convert_element_type.55
  3.8 18.4 %shard_map.86 = (bf16[16,4,384]{2,1,0:T(4,128)(2,1)}, bf16[16,4,512]{2,1,0:T(4,128)(2,1)}) custom-call(bf16[16,4,384]{2,1,0:T(4,128)(2,1)} %bitcast.59, bf16[16,4,512]{2,1,0:T(4,128)(2,1)} %bitcast.58), custom_call_target="tpu_custom_call" | custom-call | tf_op jit(solution)/shard_map/pallas_call | solution.py:60
  22.1 1.5 reshape.144.refs_1_
  23.6 1.4 reshape.143.refs_0_
  25.1 196.0 %shard_map.87 = (bf16[32,64,384]{2,1,0:T(8,128)(2,1)}, bf16[32,64,512]{2,1,0:T(8,128)(2,1)}) custom-call(bf16[64,384]{1,0:T(8,128)(2,1)} %reshape.143.refs_0_, bf16[64,512]{1,0:T(8,128)(2,1)} %reshape.144.refs_1_), custom_call_target="tpu_custom_call" | custom-call | tf_op jit(solution)/shard_map/pallas_call | solution.py:60
  221.1 0.0 copy-start.5
  221.1 1.1 convert_reduce_fusion.1
  222.2 1.1 fusion.19
  223.3 1.6 fusion.20.refs_0_
  225.0 148.5 %shard_map.85 = bf16[16,24,2048]{2,1,0:T(8,128)(2,1)} custom-call(bf16[24,2048]{1,0:T(8,128)(2,1)} %fusion.20.refs_0_), custom_call_target="tpu_custom_call" | custom-call | tf_op jit(solution)/shard_map/pallas_call | solution.py:60
  373.5 0.0 copy-done.5
  373.5 0.0 copy-start.3
  373.5 2.5 convolution_convert_fusion.1
  376.0 0.4 fusion.31
  376.4 0.1 fusion.12
  376.5 2.0 convolution_convert_fusion
  378.5 71.4 %shard_map.88 = bf16[16,24,2048]{2,1,0:T(8,128)(2,1)} custom-call(bf16[16,24,2048]{2,1,0:T(8,128)(2,1)} %bitcast.53), custom_call_target="tpu_custom_call" | custom-call | tf_op jit(solution)/shard_map/pallas_call | solution.py:60
  449.9 0.0 copy-start.1
  449.9 1.7 convert_reduce_fusion
  451.7 0.1 fusion.24
  451.8 0.2 multiply_reduce_fusion
  452.0 0.7 multiply_convert_fusion
  452.8 37.6 %shard_map.89 = bf16[16,24,2048]{2,1,0:T(8,128)(2,1)} custom-call(bf16[24,2048]{1,0:T(8,128)(2,1)} %get-tuple-element.19.refs_0_), custom_call_target="tpu_custom_call" | custom-call | tf_op jit(solution)/shard_map/pallas_call | solution.py:60
  490.3 3.3 fusion.10
  493.6 0.1 copy.14
  493.8 0.1 copy.15
  493.9 0.3 copy-done.6
  494.3 0.8 scatter_fusion
  495.1 0.0 copy-start.2
  495.1 0.7 copy-done.2
  (16 shorter events, 0.1 us)
Async XLA Ops:
  0.6 375.9 %copy-start = (bf16[128,2048]{1,0:T(8,128)(2,1)S(1)}, bf16[128,2048]{1,0:T(8,128)(2,1)}, u32[]{:S(2)}) copy-start(bf16[128,2048]{1,0:T(8,128)(2,1)} %param.11) | copy-start | bytes 1572868
  221.1 152.4 %copy-start.5 = (bf16[32,64,384]{2,1,0:T(8,128)(2,1)S(1)}, bf16[32,64,384]{2,1,0:T(8,128)(2,1)}, u32[]{:S(2)}) copy-start(bf16[32,64,384]{2,1,0:T(8,128)(2,1)} %get-tuple-element.9) | copy-start | bytes 4718596
  373.5 2.5 copy-start.3
  449.9 1.7 copy-start.1
  451.6 38.7 %copy-start.4 = (bf16[32,64,512]{2,1,0:T(8,128)(2,1)S(1)}, bf16[32,64,512]{2,1,0:T(8,128)(2,1)}, u32[]{:S(2)}) copy-start(bf16[32,64,512]{2,1,0:T(8,128)(2,1)} %get-tuple-element.10) | copy-start | bytes 6291460
  493.6 0.7 copy-start.6
  495.1 0.7 copy-start.2

commit v3 on v2

--- a/solution.py
+++ b/solution.py
@@ -11,6 +11,7 @@
 HD = 128
 PAGE = 128
 MESH = pl.DeviceIdType.MESH
+RING = 4
 
 
 def layer_norm(values):
@@ -70,6 +71,153 @@
     )(*xs)
 
 
+def _remote(src, dst, send_sem, recv_sem, axis, peer):
+    return pltpu.make_async_remote_copy(
+        src_ref=src,
+        dst_ref=dst,
+        send_sem=send_sem,
+        recv_sem=recv_sem,
+        device_id={axis: peer},
+        device_id_type=MESH,
+    )
+
+
+def dp_gather_kernel(lines, ring, x_ref, o_ref, send_sem, recv_sem):
+    me = lax.axis_index("dp")
+    z, y = me // ring, me % ring
+    barrier = pltpu.get_barrier_semaphore()
+    has_left, has_right = z > 0, z < lines - 1
+
+    def signal(peer):
+        pl.semaphore_signal(barrier, inc=1, device_id={"dp": peer}, device_id_type=MESH)
+
+    pl.when(has_left)(lambda: signal(me - ring))
+    pl.when(has_right)(lambda: signal(me + ring))
+    for k in range(1, ring):
+        signal(z * ring + (y + k) % ring)
+    n_line = has_left.astype(jnp.int32) + has_right.astype(jnp.int32)
+    pl.semaphore_wait(barrier, n_line + (ring - 1))
+
+    sends = []
+    counter = [0]
+
+    def send(cond, src, src_z, peer):
+        slot = src_z * ring + y
+        copy = _remote(src, o_ref.at[src_z, y], send_sem.at[counter[0]], recv_sem.at[slot], "dp", peer)
+        counter[0] += 1
+        pl.when(cond)(copy.start)
+        sends.append((cond, copy))
+
+    def spread(cond, src, src_z):
+        for k in range(1, ring):
+            send(cond, src, src_z, z * ring + (y + k) % ring)
+
+    def arrive(cond, src_z, peer):
+        slot = src_z * ring + y
+        copy = _remote(o_ref.at[src_z, y], o_ref.at[src_z, y], send_sem.at[0], recv_sem.at[slot], "dp", peer)
+        pl.when(cond)(copy.wait_recv)
+
+    true = z >= 0
+    send(has_right, x_ref, z, me + ring)
+    send(has_left, x_ref, z, me - ring)
+    spread(true, x_ref, z)
+    o_ref[z, y] = x_ref[...]
+    for s in range(1, lines):
+        from_left = z - s >= 0
+        src_l = jnp.maximum(z - s, 0)
+        arrive(from_left, src_l, me - ring)
+        send(from_left & has_right, o_ref.at[src_l, y], src_l, me + ring)
+        spread(from_left, o_ref.at[src_l, y], src_l)
+        from_right = z + s <= lines - 1
+        src_r = jnp.minimum(z + s, lines - 1)
+        arrive(from_right, src_r, me + ring)
+        send(from_right & has_left, o_ref.at[src_r, y], src_r, me - ring)
+        spread(from_right, o_ref.at[src_r, y], src_r)
+    for k in range(1, ring):
+        yy = (y + k) % ring
+        for zz in range(lines):
+            slot = zz * ring + yy
+            copy = _remote(o_ref.at[zz, yy], o_ref.at[zz, yy], send_sem.at[0], recv_sem.at[slot], "dp", z * ring + yy)
+            copy.wait_recv()
+    for cond, copy in sends:
+        pl.when(cond)(copy.wait_send)
+
+
+def dp_gather(x, lines, ring, cid):
+    n_sends = 1 + ring + (lines - 1) * 2 * ring
+    return pl.pallas_call(
+        functools.partial(dp_gather_kernel, lines, ring),
+        out_shape=jax.ShapeDtypeStruct((lines, ring) + x.shape, x.dtype),
+        in_specs=[pl.BlockSpec(memory_space=pltpu.VMEM)],
+        out_specs=pl.BlockSpec(memory_space=pltpu.VMEM),
+        scratch_shapes=[
+            pltpu.SemaphoreType.DMA((n_sends,)),
+            pltpu.SemaphoreType.DMA((lines * ring,)),
+        ],
+        compiler_params=pltpu.CompilerParams(collective_id=cid, has_side_effects=True),
+    )(x)
+
+
+def mp_gather_kernel(halves, chips, cores, x_ref, o_ref, send_sem, recv_sem):
+    me = lax.axis_index("mp")
+    h, c, k = me // (chips * cores), (me // cores) % chips, me % cores
+    per_half = chips * cores
+    barrier = pltpu.get_barrier_semaphore()
+    far = (1 - h) * per_half + c * cores + k
+    twin = h * per_half + c * cores + (1 - k)
+    mates = [h * per_half + ((c + j) % chips) * cores + k for j in range(1, chips)]
+    for peer in [far, twin] + mates:
+        pl.semaphore_signal(barrier, inc=1, device_id={"mp": peer}, device_id_type=MESH)
+    pl.semaphore_wait(barrier, 2 + len(mates))
+
+    sends = []
+
+    def send(src, hh, cc, kk, peer):
+        slot = (hh * chips + cc) * cores + kk
+        copy = _remote(src, o_ref.at[hh, cc, kk], send_sem.at[len(sends)], recv_sem.at[slot], "mp", peer)
+        copy.start()
+        sends.append(copy)
+
+    def arrive(hh, cc, kk, peer):
+        slot = (hh * chips + cc) * cores + kk
+        copy = _remote(o_ref.at[hh, cc, kk], o_ref.at[hh, cc, kk], send_sem.at[0], recv_sem.at[slot], "mp", peer)
+        copy.wait_recv()
+
+    send(x_ref, h, c, k, far)
+    for peer in mates:
+        send(x_ref, h, c, k, peer)
+    send(x_ref, h, c, k, twin)
+    o_ref[h, c, k] = x_ref[...]
+    arrive(1 - h, c, k, far)
+    for peer in mates:
+        send(o_ref.at[1 - h, c, k], 1 - h, c, k, peer)
+    send(o_ref.at[1 - h, c, k], 1 - h, c, k, twin)
+    for j in range(1, chips):
+        cc = (c + j) % chips
+        for hh in (h, 1 - h):
+            arrive(hh, cc, k, mates[j - 1])
+            send(o_ref.at[hh, cc, k], hh, cc, k, twin)
+    for hh in range(2):
+        for cc in range(chips):
+            arrive(hh, cc, 1 - k, twin)
+    for copy in sends:
+        copy.wait_send()
+
+
+def mp_gather(x, chips, cid):
+    return pl.pallas_call(
+        functools.partial(mp_gather_kernel, 2, chips, 2),
+        out_shape=jax.ShapeDtypeStruct((2, chips, 2) + x.shape, x.dtype),
+        in_specs=[pl.BlockSpec(memory_space=pltpu.VMEM)],
+        out_specs=pl.BlockSpec(memory_space=pltpu.VMEM),
+        scratch_shapes=[
+            pltpu.SemaphoreType.DMA((2 * chips * 2,)),
+            pltpu.SemaphoreType.DMA((2 * chips * 2,)),
+        ],
+        compiler_params=pltpu.CompilerParams(collective_id=cid, has_side_effects=True),
+    )(x)
+
+
 def attend(normed, qkv_w, segment, table, mp_index):
     group_rows = normed.shape[0]
     heads_dev = qkv_w.shape[1] // (3 * HD)
@@ -107,23 +255,24 @@
     qkv_t = qkv_master.astype(jnp.bfloat16).reshape(rows_w, mp_count, -1).transpose(1, 0, 2)
     up_t = up_master.astype(jnp.bfloat16).reshape(rows_w, mp_count, -1).transpose(1, 0, 2)
     qkv_blk, up_blk = exchange([qkv_t, up_t], "mp", True, 0)
-    qkv_g, up_g = exchange(
-        [qkv_blk.reshape(mp_count * rows_w, -1), up_blk.reshape(mp_count * rows_w, -1)],
-        "dp",
-        False,
-        1,
-    )
-    qkv_w = qkv_g.reshape(-1, qkv_g.shape[-1])
-    up_w = up_g.reshape(-1, up_g.shape[-1])
+    dp_count = lax.axis_size("dp")
+    width = qkv_t.shape[-1]
+    both = jnp.concatenate(
+        [qkv_blk.reshape(mp_count * rows_w, -1), up_blk.reshape(mp_count * rows_w, -1)], axis=1
+    )
+    gathered = dp_gather(both, dp_count // RING, RING, 1)
+    gathered = gathered.reshape(-1, gathered.shape[-1])
+    qkv_w = gathered[:, :width]
+    up_w = gathered[:, width:]
     rows = hidden_in.shape[0]
     normed_own = layer_norm(hidden_in.astype(jnp.float32)).astype(jnp.bfloat16)
-    normed = exchange([normed_own], "mp", False, 2)[0].reshape(mp_count * rows, -1)
+    normed = mp_gather(normed_own, mp_count // 4, 2).reshape(mp_count * rows, -1)
     context, cache = attend(normed, qkv_w, segment_ids[0], page_table[0], mp_index)
     partial = jnp.dot(context, dense_weight, preferred_element_type=jnp.float32).astype(jnp.bfloat16)
     parts = exchange([partial.reshape(mp_count, rows, -1)], "mp", True, 3)[0]
     share = jnp.sum(parts.astype(jnp.float32), axis=0)
     stream_own = hidden_in.astype(jnp.float32) + share
-    normed_two = exchange([layer_norm(stream_own).astype(jnp.bfloat16)], "mp", False, 4)[0]
+    normed_two = mp_gather(layer_norm(stream_own).astype(jnp.bfloat16), mp_count // 4, 4)
     normed_two = normed_two.reshape(mp_count * rows, -1)
     upper = jnp.dot(normed_two, up_w, preferred_element_type=jnp.float32)
     activated = jax.nn.gelu(upper, approximate=True).astype(jnp.bfloat16)

time: 497 us -> 243 us (0.49)
  the two profiles are of different devices: /device:TPU:239 before, /device:TPU:69 now
where the time goes in v3:
time: 243 us
  Pallas kernels  218 us (90%)
  other arithmetic  11.9 us (5%)
  matrix products  8.77 us (4%)
  local copies, waits for them, and re-layouts  2.84 us (1%)
    pallas_call x2, Pallas kernels, exchange(): pl.pallas_call(functools.partial(exchange_kernel, n, axis, spread, count)...  108 us
    pallas_call x2, Pallas kernels, mp_gather(): pl.pallas_call(functools.partial(mp_gather_kernel, 2, chips, 2), out_shap...  62 us
    pallas_call x1, Pallas kernels, dp_gather(): pl.pallas_call(functools.partial(dp_gather_kernel, lines, ring), out_shap...  48.8 us

profile of v3, /device:TPU:69, one launch (start us, length us, event | category | flops | bytes accessed | tf_op | source)
XLA Modules:
  0.0 242.7 jit_solution(10049733262091434173)
XLA Ops:
  0.6 0.0 copy-start
  0.7 0.7 fusion.37
  1.4 1.0 convert_reduce_fusion.1
  2.4 1.1 fusion.30
  3.5 0.7 reduce.4
  4.2 1.5 convert_element_type.55
  5.8 1.6 convert_element_type.56
  7.3 21.3 %shard_map.86 = (bf16[16,4,384]{2,1,0:T(4,128)(2,1)}, bf16[16,4,512]{2,1,0:T(4,128)(2,1)}) custom-call(bf16[16,4,384]{2,1,0:T(4,128)(2,1)} %bitcast.59, bf16[16,4,512]{2,1,0:T(4,128)(2,1)} %bitcast.58), custom_call_target="tpu_custom_call" | custom-call | tf_op jit(solution)/shard_map/pallas_call | solution.py:61
  28.7 0.8 reshape.140
  29.5 0.9 reshape.141
  30.4 0.7 pad_maximum_fusion.1.x_ref
  31.0 1.6 fusion.31.x_ref
  32.6 32.4 %shard_map.85 = bf16[2,4,2,24,2048]{4,3,2,1,0:T(8,128)(2,1)} custom-call(bf16[24,2048]{1,0:T(8,128)(2,1)} %fusion.31.x_ref), custom_call_target="tpu_custom_call" | custom-call | tf_op jit(solution)/shard_map/pallas_call | solution.py:208
  65.0 0.0 copy-start.2
  65.1 48.8 %shard_map.87 = bf16[8,4,64,896]{3,2,1,0:T(8,128)(2,1)} custom-call(bf16[64,896]{1,0:T(8,128)(2,1)} %pad_maximum_fusion.1.x_ref), custom_call_target="tpu_custom_call" | custom-call | tf_op jit(solution)/shard_map/pallas_call | solution.py:148
  113.9 0.0 copy-done.2
  113.9 2.4 %fusion.6 = bf16[384,384]{0,1:T(8,128)(2,1)S(1)} fusion(bf16[384,2048]{1,0:T(8,128)(2,1)S(1)} %bitcast.54, bf16[2048,896]{1,0:T(8,128)(2,1)} %bitcast.51), kind=kOutput, calls=%fused_computation.10 | convolution fusion | flops 604127232 | bytes 3440640 | tf_op jit(solution)/shard_map/dot_general | solution.py:224
  116.3 0.1 copy.15
  116.5 0.1 copy.14
  116.7 0.8 scatter_fusion
  117.5 0.0 copy-start.3
  117.5 0.4 fusion.42
  117.9 0.1 fusion.23
  118.1 2.0 convolution_convert_fusion
  120.0 86.2 %shard_map.88 = bf16[16,24,2048]{2,1,0:T(8,128)(2,1)} custom-call(bf16[16,24,2048]{2,1,0:T(8,128)(2,1)} %bitcast.53), custom_call_target="tpu_custom_call" | custom-call | tf_op jit(solution)/shard_map/pallas_call | solution.py:61
  206.3 0.0 copy-start.1
  206.3 1.7 convert_reduce_fusion
  208.0 0.1 fusion.35
  208.2 0.2 multiply_reduce_fusion
  208.4 0.7 multiply_convert_fusion
  209.1 29.6 %shard_map.89 = bf16[2,4,2,24,2048]{4,3,2,1,0:T(8,128)(2,1)} custom-call(bf16[24,2048]{1,0:T(8,128)(2,1)} %get-tuple-element.15.x_ref), custom_call_target="tpu_custom_call" | custom-call | tf_op jit(solution)/shard_map/pallas_call | solution.py:208
  238.7 3.9 %fusion.19 = bf16[384,512]{1,0:T(8,128)(2,1)} fusion(bf16[384,2048]{1,0:T(8,128)(2,1)} %bitcast.55, bf16[2048,896]{1,0:T(8,128)(2,1)} %bitcast.52), kind=kOutput, calls=%fused_computation.21 | convolution fusion | flops 807075840 | bytes 4063232 | tf_op jit(solution)/shard_map/dot_general | solution.py:277
  (11 shorter events, 0.1 us)
Async XLA Ops:
  0.6 117.4 %copy-start = (bf16[128,2048]{1,0:T(8,128)(2,1)S(1)}, bf16[128,2048]{1,0:T(8,128)(2,1)}, u32[]{:S(2)}) copy-start(bf16[128,2048]{1,0:T(8,128)(2,1)} %param.11) | copy-start | bytes 1572868
  65.0 48.8 %copy-start.2 = (bf16[2,4,2,24,2048]{4,3,2,1,0:T(8,128)(2,1)S(1)}, bf16[2,4,2,24,2048]{4,3,2,1,0:T(8,128)(2,1)}, u32[]{:S(2)}) copy-start(bf16[2,4,2,24,2048]{4,3,2,1,0:T(8,128)(2,1)} %shard_map.85) | copy-start | bytes 4718596
  117.5 2.5 %copy-start.3 = (bf16[3,2,128,128]{3,2,1,0:T(8,128)(2,1)}, bf16[3,2,128,128]{3,2,1,0:T(8,128)(2,1)S(1)}, u32[]{:S(2)}) copy-start(bf16[3,2,128,128]{3,2,1,0:T(8,128)(2,1)S(1)} %scatter_fusion) | copy-start | bytes 589828
  206.3 1.7 copy-start.1

commit v4 on v3

--- a/solution.py
+++ b/solution.py
@@ -218,6 +218,77 @@
     )(x)
 
 
+def mp_sum_kernel(chips, p_ref, o_ref, twin_in, pair, mate_in, far_out, far_in, acc, send_sem, recv_sem):
+    me = lax.axis_index("mp")
+    per_half = chips * 2
+    h, c, k = me // per_half, (me // 2) % chips, me % 2
+    far = (1 - h) * per_half + c * 2 + k
+    twin = h * per_half + c * 2 + (1 - k)
+    mates = [h * per_half + ((c + j) % chips) * 2 + k for j in range(1, chips)]
+    barrier = pltpu.get_barrier_semaphore()
+    for peer in [far, twin] + mates:
+        pl.semaphore_signal(barrier, inc=1, device_id={"mp": peer}, device_id_type=MESH)
+    pl.semaphore_wait(barrier, 2 + len(mates))
+
+    sends = []
+
+    def send(src, dst, slot, peer):
+        copy = _remote(src, dst, send_sem.at[len(sends)], recv_sem.at[slot], "mp", peer)
+        copy.start()
+        sends.append(copy)
+
+    def arrive(dst, slot, peer):
+        _remote(dst, dst, send_sem.at[0], recv_sem.at[slot], "mp", peer).wait_recv()
+
+    for hh in range(2):
+        for cc in range(chips):
+            send(p_ref.at[hh, cc, 1 - k], twin_in.at[hh, cc], hh * chips + cc, twin)
+    for j in range(1, chips):
+        cc = (c + j) % chips
+        for hh in range(2):
+            arrive(twin_in.at[hh, cc], hh * chips + cc, twin)
+            pair[hh, cc] = (
+                p_ref[hh, cc, k].astype(jnp.float32) + twin_in[hh, cc].astype(jnp.float32)
+            ).astype(pair.dtype)
+            send(pair.at[hh, cc], mate_in.at[c, hh], 2 * chips + c * 2 + hh, mates[j - 1])
+    for hh in range(2):
+        arrive(twin_in.at[hh, c], hh * chips + c, twin)
+        acc[hh] = p_ref[hh, c, k].astype(jnp.float32) + twin_in[hh, c].astype(jnp.float32)
+    for j in range(1, chips):
+        cc = (c + j) % chips
+        for hh in range(2):
+            arrive(mate_in.at[cc, hh], 2 * chips + cc * 2 + hh, mates[j - 1])
+            acc[hh] = acc[hh] + mate_in[cc, hh].astype(jnp.float32)
+    far_out[...] = acc[1 - h].astype(far_out.dtype)
+    send(far_out, far_in, 4 * chips, far)
+    arrive(far_in, 4 * chips, far)
+    o_ref[...] = acc[h] + far_in[...].astype(jnp.float32)
+    for copy in sends:
+        copy.wait_send()
+
+
+def mp_sum(parts, chips, cid):
+    rows, cols = parts.shape[-2:]
+    dt = parts.dtype
+    return pl.pallas_call(
+        functools.partial(mp_sum_kernel, chips),
+        out_shape=jax.ShapeDtypeStruct((rows, cols), jnp.float32),
+        in_specs=[pl.BlockSpec(memory_space=pltpu.VMEM)],
+        out_specs=pl.BlockSpec(memory_space=pltpu.VMEM),
+        scratch_shapes=[
+            pltpu.VMEM((2, chips, rows, cols), dt),
+            pltpu.VMEM((2, chips, rows, cols), dt),
+            pltpu.VMEM((chips, 2, rows, cols), dt),
+            pltpu.VMEM((rows, cols), dt),
+            pltpu.VMEM((rows, cols), dt),
+            pltpu.VMEM((2, rows, cols), jnp.float32),
+            pltpu.SemaphoreType.DMA((4 * chips + 1,)),
+            pltpu.SemaphoreType.DMA((4 * chips + 1,)),
+        ],
+        compiler_params=pltpu.CompilerParams(collective_id=cid, has_side_effects=True),
+    )(parts)
+
+
 def attend(normed, qkv_w, segment, table, mp_index):
     group_rows = normed.shape[0]
     heads_dev = qkv_w.shape[1] // (3 * HD)
@@ -269,8 +340,7 @@
     normed = mp_gather(normed_own, mp_count // 4, 2).reshape(mp_count * rows, -1)
     context, cache = attend(normed, qkv_w, segment_ids[0], page_table[0], mp_index)
     partial = jnp.dot(context, dense_weight, preferred_element_type=jnp.float32).astype(jnp.bfloat16)
-    parts = exchange([partial.reshape(mp_count, rows, -1)], "mp", True, 3)[0]
-    share = jnp.sum(parts.astype(jnp.float32), axis=0)
+    share = mp_sum(partial.reshape(2, mp_count // 4, 2, rows, -1), mp_count // 4, 3)
     stream_own = hidden_in.astype(jnp.float32) + share
     normed_two = mp_gather(layer_norm(stream_own).astype(jnp.bfloat16), mp_count // 4, 4)
     normed_two = normed_two.reshape(mp_count * rows, -1)

time: 243 us -> 184 us (0.76)
  the two profiles are of different devices: /device:TPU:69 before, /device:TPU:57 now
where the time goes in v4:
time: 184 us
  Pallas kernels  161 us (88%)
  matrix products  9.24 us (5%)
  other arithmetic  8.93 us (5%)
  local copies, waits for them, and re-layouts  3.83 us (2%)
    pallas_call x2, Pallas kernels, mp_gather(): pl.pallas_call(functools.partial(mp_gather_kernel, 2, chips, 2), out_shap...  58.3 us
    pallas_call x1, Pallas kernels, dp_gather(): pl.pallas_call(functools.partial(dp_gather_kernel, lines, ring), out_shap...  47.7 us
    pallas_call x1, Pallas kernels, mp_sum(): pl.pallas_call(functools.partial(mp_sum_kernel, chips), out_shape=jax.Sha...  33.3 us
    pallas_call x1, Pallas kernels, exchange(): pl.pallas_call(functools.partial(exchange_kernel, n, axis, spread, count)...  21.7 us
    dot_general x1, matrix products, local(): upper = jnp.dot(normed_two, up_w, preferred_element_type=jnp.float32)  3.94 us

profile of v4, /device:TPU:57, one launch (start us, length us, event | category | flops | bytes accessed | tf_op | source)
XLA Modules:
  0.0 183.8 jit_solution(9810083870176741203)
XLA Ops:
  0.6 0.0 copy-start
  0.6 1.6 convert_element_type.53
  2.3 1.5 convert_element_type.52
  3.8 21.7 %shard_map.86 = (bf16[16,4,384]{2,1,0:T(4,128)(2,1)}, bf16[16,4,512]{2,1,0:T(4,128)(2,1)}) custom-call(bf16[16,4,384]{2,1,0:T(4,128)(2,1)} %bitcast.58, bf16[16,4,512]{2,1,0:T(4,128)(2,1)} %bitcast.57), custom_call_target="tpu_custom_call" | custom-call | tf_op jit(solution)/shard_map/pallas_call | solution.py:61
  25.5 0.9 reshape.141
  26.4 0.8 reshape.140
  27.2 0.7 pad_maximum_fusion.1.x_ref
  27.8 47.7 %shard_map.87 = bf16[8,4,64,896]{3,2,1,0:T(8,128)(2,1)} custom-call(bf16[64,896]{1,0:T(8,128)(2,1)} %pad_maximum_fusion.1.x_ref), custom_call_target="tpu_custom_call" | custom-call | tf_op jit(solution)/shard_map/pallas_call | solution.py:148
  75.6 0.0 copy-done.1
  75.6 0.1 convert_reduce_fusion
  75.7 0.2 fusion.30
  75.9 0.7 fusion.31.x_ref
  76.7 33.3 %shard_map.85 = bf16[2,4,2,24,2048]{4,3,2,1,0:T(8,128)(2,1)} custom-call(bf16[24,2048]{1,0:T(8,128)(2,1)} %fusion.31.x_ref), custom_call_target="tpu_custom_call" | custom-call | tf_op jit(solution)/shard_map/pallas_call | solution.py:208
  110.0 0.0 copy-start.3
  110.0 2.9 %fusion.6 = bf16[384,384]{0,1:T(8,128)(2,1)S(1)} fusion(bf16[384,2048]{1,0:T(8,128)(2,1)} %bitcast.54, bf16[2048,896]{1,0:T(8,128)(2,1)} %bitcast.50), kind=kOutput, calls=%fused_computation.9 | convolution fusion | flops 604127232 | bytes 3440640 | tf_op jit(solution)/shard_map/dot_general | solution.py:295
  113.0 0.0 copy-done.3
  113.0 0.4 fusion.42
  113.4 0.1 fusion.23
  113.5 0.0 copy-done
  113.5 2.0 %convolution_convert_fusion = bf16[384,2048]{1,0:T(8,128)(2,1)} fusion(bf16[128,2048]{1,0:T(8,128)(2,1)S(1)} %copy-done, f32[384,384]{0,1:T(8,128)S(1)} %get-tuple-element.18, f32[384]{0:T(512)S(1)} %fusion.23, f32[384]{0:T(512)S(1)} %get-tuple-element.17, bf16[384,1,3,128]{0,3,2,1:T(8,128)(2,1)S(1)} %bitcast.60), kind=kOutput, calls=%fused_computation.1 | convolution fusion | flops 240353280 | bytes 2789376 | tf_op jit(solution)/shard_map/dot_general | solution.py:342
  115.5 33.3 %shard_map.88 = f32[24,2048]{1,0:T(8,128)} custom-call(bf16[2,4,2,24,2048]{4,3,2,1,0:T(8,128)(2,1)} %bitcast.52), custom_call_target="tpu_custom_call" | custom-call | tf_op jit(solution)/shard_map/pallas_call | solution.py:273
  148.8 1.1 fusion.35
  149.8 1.1 multiply_reduce_fusion
  151.0 1.7 multiply_convert_fusion
  152.6 25.0 %shard_map.89 = bf16[2,4,2,24,2048]{4,3,2,1,0:T(8,128)(2,1)} custom-call(bf16[24,2048]{1,0:T(8,128)(2,1)} %get-tuple-element.15.x_ref), custom_call_target="tpu_custom_call" | custom-call | tf_op jit(solution)/shard_map/pallas_call | solution.py:208
  177.6 3.9 %fusion.19 = bf16[384,512]{1,0:T(8,128)(2,1)} fusion(bf16[384,2048]{1,0:T(8,128)(2,1)} %bitcast.53, bf16[2048,896]{1,0:T(8,128)(2,1)} %bitcast.51), kind=kOutput, calls=%fused_computation.20 | convolution fusion | flops 807075840 | bytes 4063232 | tf_op jit(solution)/shard_map/dot_general | solution.py:347
  181.6 0.1 copy.14
  181.7 0.1 copy.15
  181.9 0.3 copy-done.4
  182.2 0.8 scatter_fusion
  183.1 0.0 copy-start.2
  183.1 0.7 copy-done.2
  (12 shorter events, 0.1 us)
Async XLA Ops:
  0.6 112.9 %copy-start = (bf16[128,2048]{1,0:T(8,128)(2,1)S(1)}, bf16[128,2048]{1,0:T(8,128)(2,1)}, u32[]{:S(2)}) copy-start(bf16[128,2048]{1,0:T(8,128)(2,1)} %param.11) | copy-start | bytes 1572868
  27.8 47.7 %copy-start.1 = (bf16[24,2048]{1,0:T(8,128)(2,1)S(1)}, bf16[24,2048]{1,0:T(8,128)(2,1)}, u32[]{:S(2)}) copy-start(bf16[24,2048]{1,0:T(8,128)(2,1)} %param.6) | copy-start | bytes 294916
  110.0 3.0 %copy-start.3 = (s32[1,384]{1,0:T(1,128)S(1)}, s32[1,384]{1,0:T(1,128)}, u32[]{:S(2)}) copy-start(s32[1,384]{1,0:T(1,128)} %param.7) | copy-start | bytes 4612
  181.6 0.7 copy-start.4
  183.1 0.7 copy-start.2

commit v5 on v1

--- a/solution.py
+++ b/solution.py
@@ -1,11 +1,17 @@
+import functools
+
 import jax
 import jax.numpy as jnp
 from jax import lax
+from jax.experimental import pallas as pl
+from jax.experimental.pallas import tpu as pltpu
 from jax.sharding import PartitionSpec as P
 
 H = 16
 HD = 128
 PAGE = 128
+RING = 4
+MESH = pl.DeviceIdType.MESH
 
 
 def layer_norm(values):
@@ -15,10 +21,268 @@
     return centered * lax.rsqrt(variance + 1e-05)
 
 
-def gather_rows(x, axis):
-    n = lax.axis_size(axis)
-    tiled = jnp.concatenate([x] * n, axis=0)
-    return lax.all_to_all(tiled, axis, split_axis=0, concat_axis=0, tiled=True)
+def _remote(src, dst, send_sem, recv_sem, axis, peer):
+    return pltpu.make_async_remote_copy(
+        src_ref=src,
+        dst_ref=dst,
+        send_sem=send_sem,
+        recv_sem=recv_sem,
+        device_id={axis: peer},
+        device_id_type=MESH,
+    )
+
+
+def mp_places(chips):
+    me = lax.axis_index("mp")
+    per_half = chips * 2
+    h, c, k = me // per_half, (me // 2) % chips, me % 2
+    far = (1 - h) * per_half + c * 2 + k
+    twin = h * per_half + c * 2 + (1 - k)
+    mates = [h * per_half + ((c + j) % chips) * 2 + k for j in range(1, chips)]
+    return h, c, k, far, twin, mates
+
+
+def exchange_peers(n, axis):
+    me = lax.axis_index(axis)
+    return [(None, axis, lax.rem(me + step, n)) for step in range(1, n)]
+
+
+def exchange_body(n, axis, ins, outs, scratch):
+    send_sem, recv_sem, local_sem = scratch
+    me = lax.axis_index(axis)
+    copies, locals_ = [], []
+    for a in range(len(ins)):
+        for step in range(1, n):
+            peer = lax.rem(me + step, n)
+            slot = a * (n - 1) + step - 1
+            copy = _remote(ins[a].at[peer], outs[a].at[me], send_sem.at[slot], recv_sem.at[slot], axis, peer)
+            copy.start()
+            copies.append(copy)
+        own = pltpu.make_async_copy(ins[a].at[me], outs[a].at[me], local_sem.at[a])
+        own.start()
+        locals_.append(own)
+    yield
+    for own in locals_:
+        own.wait()
+    for copy in copies:
+        copy.wait()
+
+
+def exchange_scratch(n, count):
+    return [
+        pltpu.SemaphoreType.DMA((count * (n - 1),)),
+        pltpu.SemaphoreType.DMA((count * (n - 1),)),
+        pltpu.SemaphoreType.DMA((count,)),
+    ]
+
+
+def dp_peers(lines, ring):
+    me = lax.axis_index("dp")
+    z, y = me // ring, me % ring
+    out = [(z > 0, "dp", me - ring), (z < lines - 1, "dp", me + ring)]
+    return out + [(None, "dp", z * ring + (y + k) % ring) for k in range(1, ring)]
+
+
+def dp_gather_body(lines, ring, ins, outs, scratch):
+    (x_ref,), (o_ref,), (send_sem, recv_sem) = ins, outs, scratch
+    me = lax.axis_index("dp")
+    z, y = me // ring, me % ring
+    has_left, has_right = z > 0, z < lines - 1
+    sends = []
+
+    def send(cond, src, src_z, peer):
+        slot = src_z * ring + y
+        copy = _remote(src, o_ref.at[src_z, y], send_sem.at[len(sends)], recv_sem.at[slot], "dp", peer)
+        pl.when(cond)(copy.start)
+        sends.append((cond, copy))
+
+    def spread(cond, src, src_z):
+        for k in range(1, ring):
+            send(cond, src, src_z, z * ring + (y + k) % ring)
+
+    def arrive(cond, src_z, peer):
+        slot = src_z * ring + y
+        copy = _remote(o_ref.at[src_z, y], o_ref.at[src_z, y], send_sem.at[0], recv_sem.at[slot], "dp", peer)
+        pl.when(cond)(copy.wait_recv)
+
+    send(has_right, x_ref, z, me + ring)
+    send(has_left, x_ref, z, me - ring)
+    spread(z >= 0, x_ref, z)
+    o_ref[z, y] = x_ref[...]
+    yield
+    for s in range(1, lines):
+        from_left = z - s >= 0
+        src_l = jnp.maximum(z - s, 0)
+        arrive(from_left, src_l, me - ring)
+        send(from_left & has_right, o_ref.at[src_l, y], src_l, me + ring)
+        spread(from_left, o_ref.at[src_l, y], src_l)
+        from_right = z + s <= lines - 1
+        src_r = jnp.minimum(z + s, lines - 1)
+        arrive(from_right, src_r, me + ring)
+        send(from_right & has_left, o_ref.at[src_r, y], src_r, me - ring)
+        spread(from_right, o_ref.at[src_r, y], src_r)
+        yield
+    for k in range(1, ring):
+        yy = (y + k) % ring
+        for zz in range(lines):
+            slot = zz * ring + yy
+            copy = _remote(o_ref.at[zz, yy], o_ref.at[zz, yy], send_sem.at[0], recv_sem.at[slot], "dp", z * ring + yy)
+            copy.wait_recv()
+    for cond, copy in sends:
+        pl.when(cond)(copy.wait_send)
+
+
+def dp_scratch(lines, ring):
+    return [
+        pltpu.SemaphoreType.DMA((1 + ring + (lines - 1) * 2 * ring,)),
+        pltpu.SemaphoreType.DMA((lines * ring,)),
+    ]
+
+
+def mp_peers(chips):
+    _, _, _, far, twin, mates = mp_places(chips)
+    return [(None, "mp", peer) for peer in [far, twin] + mates]
+
+
+def mp_gather_body(chips, ins, outs, scratch):
+    (x_ref,), (o_ref,), (send_sem, recv_sem) = ins, outs, scratch
+    h, c, k, far, twin, mates = mp_places(chips)
+    sends = []
+
+    def send(src, hh, cc, kk, peer):
+        slot = (hh * chips + cc) * 2 + kk
+        copy = _remote(src, o_ref.at[hh, cc, kk], send_sem.at[len(sends)], recv_sem.at[slot], "mp", peer)
+        copy.start()
+        sends.append(copy)
+
+    def arrive(hh, cc, kk, peer):
+        slot = (hh * chips + cc) * 2 + kk
+        copy = _remote(o_ref.at[hh, cc, kk], o_ref.at[hh, cc, kk], send_sem.at[0], recv_sem.at[slot], "mp", peer)
+        copy.wait_recv()
+
+    send(x_ref, h, c, k, far)
+    for peer in mates:
+        send(x_ref, h, c, k, peer)
+    send(x_ref, h, c, k, twin)
+    o_ref[h, c, k] = x_ref[...]
+    yield
+    arrive(1 - h, c, k, far)
+    for peer in mates:
+        send(o_ref.at[1 - h, c, k], 1 - h, c, k, peer)
+    send(o_ref.at[1 - h, c, k], 1 - h, c, k, twin)
+    yield
+    for j in range(1, chips):
+        cc = (c + j) % chips
+        for hh in (h, 1 - h):
+            arrive(hh, cc, k, mates[j - 1])
+            send(o_ref.at[hh, cc, k], hh, cc, k, twin)
+    yield
+    for hh in range(2):
+        for cc in range(chips):
+            arrive(hh, cc, 1 - k, twin)
+    for copy in sends:
+        copy.wait_send()
+
+
+def mp_gather_scratch(chips):
+    return [pltpu.SemaphoreType.DMA((4 * chips,)), pltpu.SemaphoreType.DMA((4 * chips,))]
+
+
+def mp_sum_body(chips, ins, outs, scratch):
+    (p_ref,), (o_ref,) = ins, outs
+    twin_in, pair, mate_in, far_out, far_in, acc, send_sem, recv_sem = scratch
+    h, c, k, far, twin, mates = mp_places(chips)
+    sends = []
+
+    def send(src, dst, slot, peer):
+        copy = _remote(src, dst, send_sem.at[len(sends)], recv_sem.at[slot], "mp", peer)
+        copy.start()
+        sends.append(copy)
+
+    def arrive(dst, slot, peer):
+        _remote(dst, dst, send_sem.at[0], recv_sem.at[slot], "mp", peer).wait_recv()
+
+    for hh in range(2):
+        for cc in range(chips):
+            send(p_ref.at[hh, cc, 1 - k], twin_in.at[hh, cc], hh * chips + cc, twin)
+    yield
+    for j in range(1, chips):
+        cc = (c + j) % chips
+        for hh in range(2):
+            arrive(twin_in.at[hh, cc], hh * chips + cc, twin)
+            pair[hh, cc] = (
+                p_ref[hh, cc, k].astype(jnp.float32) + twin_in[hh, cc].astype(jnp.float32)
+            ).astype(pair.dtype)
+            send(pair.at[hh, cc], mate_in.at[c, hh], 2 * chips + c * 2 + hh, mates[j - 1])
+    for hh in range(2):
+        arrive(twin_in.at[hh, c], hh * chips + c, twin)
+        acc[hh] = p_ref[hh, c, k].astype(jnp.float32) + twin_in[hh, c].astype(jnp.float32)
+    yield
+    for j in range(1, chips):
+        cc = (c + j) % chips
+        for hh in range(2):
+            arrive(mate_in.at[cc, hh], 2 * chips + cc * 2 + hh, mates[j - 1])
+            acc[hh] = acc[hh] + mate_in[cc, hh].astype(jnp.float32)
+    far_out[...] = acc[1 - h].astype(far_out.dtype)
+    send(far_out, far_in, 4 * chips, far)
+    yield
+    arrive(far_in, 4 * chips, far)
+    o_ref[...] = acc[h] + far_in[...].astype(jnp.float32)
+    for copy in sends:
+        copy.wait_send()
+
+
+def mp_sum_scratch(chips, rows, cols, dt):
+    return [
+        pltpu.VMEM((2, chips, rows, cols), dt),
+        pltpu.VMEM((2, chips, rows, cols), dt),
+        pltpu.VMEM((chips, 2, rows, cols), dt),
+        pltpu.VMEM((rows, cols), dt),
+        pltpu.VMEM((rows, cols), dt),
+        pltpu.VMEM((2, rows, cols), jnp.float32),
+        pltpu.SemaphoreType.DMA((4 * chips + 1,)),
+        pltpu.SemaphoreType.DMA((4 * chips + 1,)),
+    ]
+
+
+def combined_kernel(parts, *refs):
+    n_in = sum(p[2] for p in parts)
+    n_out = sum(p[3] for p in parts)
+    ins, outs, scratch = refs[:n_in], refs[n_in:n_in + n_out], refs[n_in + n_out:]
+    barrier = pltpu.get_barrier_semaphore()
+    total = 0
+    for peers, _, _, _, _ in parts:
+        for cond, axis, peer in peers():
+            def signal(axis=axis, peer=peer):
+                pl.semaphore_signal(barrier, inc=1, device_id={axis: peer}, device_id_type=MESH)
+            if cond is None:
+                signal()
+                total = total + 1
+            else:
+                pl.when(cond)(signal)
+                total = total + cond.astype(jnp.int32)
+    pl.semaphore_wait(barrier, total)
+    gens = []
+    for _, body, pi, po, ps in parts:
+        gens.append(body(ins[:pi], outs[:po], scratch[:ps]))
+        ins, outs, scratch = ins[pi:], outs[po:], scratch[ps:]
+    while gens:
+        for gen in list(gens):
+            try:
+                next(gen)
+            except StopIteration:
+                gens.remove(gen)
+
+
+def combined(parts, inputs, out_shapes, scratch_shapes, cid):
+    return pl.pallas_call(
+        functools.partial(combined_kernel, parts),
+        out_shape=out_shapes,
+        in_specs=[pl.BlockSpec(memory_space=pltpu.VMEM)] * len(inputs),
+        out_specs=[pl.BlockSpec(memory_space=pltpu.VMEM)] * len(out_shapes),
+        scratch_shapes=scratch_shapes,
+        compiler_params=pltpu.CompilerParams(collective_id=cid, has_side_effects=True),
+    )(*inputs)
 
 
 def attend(normed, qkv_w, segment, table, mp_index):
@@ -53,27 +317,68 @@
 
 def local(hidden_in, segment_ids, page_table, qkv_master, up_master, dense_weight):
     mp_count = lax.axis_size("mp")
+    dp_count = lax.axis_size("dp")
     mp_index = lax.axis_index("mp")
-    qkv_bf = qkv_master.astype(jnp.bfloat16)
-    up_bf = up_master.astype(jnp.bfloat16)
-    qkv_w = gather_rows(
-        lax.all_to_all(qkv_bf, "mp", split_axis=1, concat_axis=0, tiled=True), "dp"
-    )
-    up_w = gather_rows(
-        lax.all_to_all(up_bf, "mp", split_axis=1, concat_axis=0, tiled=True), "dp"
-    )
-    normed_own = layer_norm(hidden_in.astype(jnp.float32)).astype(jnp.bfloat16)
-    normed = gather_rows(normed_own, "mp")
+    chips = mp_count // 4
+    lines = dp_count // RING
+    rows = hidden_in.shape[0]
+    rows_w = qkv_master.shape[0]
+    bf = jnp.bfloat16
+    qkv_t = qkv_master.astype(bf).reshape(rows_w, mp_count, -1).transpose(1, 0, 2)
+    up_t = up_master.astype(bf).reshape(rows_w, mp_count, -1).transpose(1, 0, 2)
+    normed_own = layer_norm(hidden_in.astype(jnp.float32)).astype(bf)
+    sd = jax.ShapeDtypeStruct
+    qkv_blk, up_blk, normed = combined(
+        [
+            (
+                functools.partial(exchange_peers, mp_count, "mp"),
+                functools.partial(exchange_body, mp_count, "mp"),
+                2, 2, 3,
+            ),
+            (functools.partial(mp_peers, chips), functools.partial(mp_gather_body, chips), 1, 1, 2),
+        ],
+        [qkv_t, up_t, normed_own],
+        [sd(qkv_t.shape, bf), sd(up_t.shape, bf), sd((2, chips, 2) + normed_own.shape, bf)],
+        exchange_scratch(mp_count, 2) + mp_gather_scratch(chips),
+        0,
+    )
+    normed = normed.reshape(mp_count * rows, -1)
+    qkv_piece = qkv_blk.reshape(mp_count * rows_w, -1)
+    up_piece = up_blk.reshape(mp_count * rows_w, -1)
+    (qkv_w,) = combined(
+        [(functools.partial(dp_peers, lines, RING), functools.partial(dp_gather_body, lines, RING), 1, 1, 2)],
+        [qkv_piece],
+        [sd((lines, RING) + qkv_piece.shape, bf)],
+        dp_scratch(lines, RING),
+        1,
+    )
+    qkv_w = qkv_w.reshape(-1, qkv_piece.shape[-1])
     context, cache = attend(normed, qkv_w, segment_ids[0], page_table[0], mp_index)
-    partial = jnp.dot(context, dense_weight, preferred_element_type=jnp.float32).astype(jnp.bfloat16)
-    parts = lax.all_to_all(partial, "mp", split_axis=0, concat_axis=0, tiled=True)
-    rows = hidden_in.shape[0]
-    share = jnp.sum(parts.reshape(mp_count, rows, -1).astype(jnp.float32), axis=0)
+    partial = jnp.dot(context, dense_weight, preferred_element_type=jnp.float32).astype(bf)
+    share, up_w = combined(
+        [
+            (functools.partial(mp_peers, chips), functools.partial(mp_sum_body, chips), 1, 1, 8),
+            (functools.partial(dp_peers, lines, RING), functools.partial(dp_gather_body, lines, RING), 1, 1, 2),
+        ],
+        [partial.reshape(2, chips, 2, rows, -1), up_piece],
+        [sd((rows, partial.shape[-1]), jnp.float32), sd((lines, RING) + up_piece.shape, bf)],
+        mp_sum_scratch(chips, rows, partial.shape[-1], bf) + dp_scratch(lines, RING),
+        2,
+    )
+    up_w = up_w.reshape(-1, up_piece.shape[-1])
     stream_own = hidden_in.astype(jnp.float32) + share
-    normed_two = gather_rows(layer_norm(stream_own).astype(jnp.bfloat16), "mp")
+    normed_two_own = layer_norm(stream_own).astype(bf)
+    (normed_two,) = combined(
+        [(functools.partial(mp_peers, chips), functools.partial(mp_gather_body, chips), 1, 1, 2)],
+        [normed_two_own],
+        [sd((2, chips, 2) + normed_two_own.shape, bf)],
+        mp_gather_scratch(chips),
+        3,
+    )
+    normed_two = normed_two.reshape(mp_count * rows, -1)
     upper = jnp.dot(normed_two, up_w, preferred_element_type=jnp.float32)
-    activated = jax.nn.gelu(upper, approximate=True).astype(jnp.bfloat16)
-    return (stream_own.astype(jnp.bfloat16), activated, cache)
+    activated = jax.nn.gelu(upper, approximate=True).astype(bf)
+    return (stream_own.astype(bf), activated, cache)
 
 
 def solution(mesh):

time: 510 us -> 179 us (0.35)
  the two profiles are of different devices: /device:TPU:33 before, /device:TPU:1 now
where the time goes in v5:
time: 179 us; the launch traced here: 178 us
  Pallas kernels  153 us (85%)
  other arithmetic  12.4 us (7%)
  matrix products  8.1 us (5%)
  local copies, waits for them, and re-layouts  4.21 us (2%)
    pallas_call x4, Pallas kernels, combined(): pl.pallas_call(functools.partial(combined_kernel, parts), out_shape=out_s...  153 us

profile of v5, /device:TPU:1, one launch (start us, length us, event | category | flops | bytes accessed | tf_op | source)
XLA Modules:
  0.0 178.4 jit_solution(3874878366023929172)
XLA Ops:
  0.6 0.0 copy-start
  0.7 0.7 fusion.26
  1.4 1.0 convert_reduce_fusion
  2.4 1.1 fusion.19
  3.5 0.7 reduce.4
  4.2 1.5 convert_element_type.51
  5.8 1.6 convert_element_type.52
  7.3 1.6 fusion.20.refs_2_
  8.9 34.9 %shard_map.85 = (bf16[16,4,384]{2,1,0:T(4,128)(2,1)}, bf16[16,4,512]{2,1,0:T(4,128)(2,1)}, bf16[2,4,2,24,2048]{4,3,2,1,0:T(8,128)(2,1)}) custom-call(bf16[16,4,384]{2,1,0:T(4,128)(2,1)} %bitcast.60, bf16[16,4,512]{2,1,0:T(4,128)(2,1)} %bitcast.59, bf16[24,2048]{1,0:T(8,128)(2,1)} %fusion.20.refs_2_), custom_call_target="tpu_custom_call" | custom-call | tf_op jit(solution)/shard_map/pallas_call | solution.py:278
  43.9 0.0 copy-start.4
  43.9 1.6 reshape.143.refs_0_
  45.5 1.5 reshape.151.refs_1_
  47.0 37.8 %shard_map.86 = bf16[8,4,64,384]{3,2,1,0:T(8,128)(2,1)} custom-call(bf16[64,384]{1,0:T(8,128)(2,1)} %reshape.143.refs_0_), custom_call_target="tpu_custom_call" | custom-call | tf_op jit(solution)/shard_map/pallas_call | solution.py:278
  84.7 0.0 copy-done.4
  84.7 2.5 %convolution_convert_fusion.1 = bf16[384,384]{0,1:T(8,128)(2,1)S(1)} fusion(bf16[384,2048]{1,0:T(8,128)(2,1)S(1)} %bitcast.65, bf16[2048,384]{1,0:T(8,128)(2,1)} %bitcast.55), kind=kOutput, calls=%fused_computation.5 | convolution fusion | flops 604127232 | bytes 3440640 | tf_op jit(solution)/shard_map/dot_general | solution.py:291
  87.2 0.1 copy.15
  87.4 0.1 copy.14
  87.6 0.8 scatter_fusion
  88.4 0.0 copy-start.2
  88.4 0.4 fusion.31
  88.8 0.1 fusion.12
  89.0 0.0 copy-done
  89.0 2.0 %convolution_convert_fusion = bf16[384,2048]{1,0:T(8,128)(2,1)} fusion(bf16[128,2048]{1,0:T(8,128)(2,1)S(1)} %copy-done, f32[384,384]{0,1:T(8,128)S(1)} %get-tuple-element.24, f32[384]{0:T(512)S(1)} %fusion.12, f32[384]{0:T(512)S(1)} %get-tuple-element.23, bf16[384,1,3,128]{0,3,2,1:T(8,128)(2,1)S(1)} %bitcast.63), kind=kOutput, calls=%fused_computation.1 | convolution fusion | flops 240353280 | bytes 2789376 | tf_op jit(solution)/shard_map/dot_general | solution.py:357
  90.9 0.0 copy-done.2
  90.9 56.3 %shard_map.87 = (f32[24,2048]{1,0:T(8,128)}, bf16[8,4,64,512]{3,2,1,0:T(8,128)(2,1)}) custom-call(bf16[2,4,2,24,2048]{4,3,2,1,0:T(8,128)(2,1)} %bitcast.54, bf16[64,512]{1,0:T(8,128)(2,1)} %reshape.151.refs_1_), custom_call_target="tpu_custom_call" | custom-call | tf_op jit(solution)/shard_map/pallas_call | solution.py:278
  147.2 0.0 copy-start.3
  147.2 0.0 copy-done.1
  147.2 1.2 fusion.24
  148.4 1.1 multiply_reduce_fusion
  149.6 1.7 multiply_convert_fusion
  151.2 23.8 %shard_map.88 = bf16[2,4,2,24,2048]{4,3,2,1,0:T(8,128)(2,1)} custom-call(bf16[24,2048]{1,0:T(8,128)(2,1)} %get-tuple-element.21.refs_0_), custom_call_target="tpu_custom_call" | custom-call | tf_op jit(solution)/shard_map/pallas_call | solution.py:278
  175.1 3.3 %fusion.10 = bf16[384,512]{1,0:T(8,128)(2,1)} fusion(bf16[384,2048]{1,0:T(8,128)(2,1)} %bitcast.56, bf16[2048,512]{1,0:T(8,128)(2,1)S(1)} %bitcast.64), kind=kOutput, calls=%fused_computation.16 | convolution fusion | flops 807075840 | bytes 4063232 | tf_op jit(solution)/shard_map/dot_general | solution.py:379
  (10 shorter events, 0.1 us)
Async XLA Ops:
  0.6 88.3 %copy-start = (bf16[128,2048]{1,0:T(8,128)(2,1)S(1)}, bf16[128,2048]{1,0:T(8,128)(2,1)}, u32[]{:S(2)}) copy-start(bf16[128,2048]{1,0:T(8,128)(2,1)} %param.11) | copy-start | bytes 1572868
  43.9 40.8 %copy-start.4 = (bf16[2,4,2,24,2048]{4,3,2,1,0:T(8,128)(2,1)S(1)}, bf16[2,4,2,24,2048]{4,3,2,1,0:T(8,128)(2,1)}, u32[]{:S(2)}) copy-start(bf16[2,4,2,24,2048]{4,3,2,1,0:T(8,128)(2,1)} %get-tuple-element.8) | copy-start | bytes 4718596
  88.4 2.5 %copy-start.2 = (bf16[3,2,128,128]{3,2,1,0:T(8,128)(2,1)}, bf16[3,2,128,128]{3,2,1,0:T(8,128)(2,1)S(1)}, u32[]{:S(2)}) copy-start(bf16[3,2,128,128]{3,2,1,0:T(8,128)(2,1)S(1)} %scatter_fusion) | copy-start | bytes 589828
  90.9 56.3 %copy-start.1 = (bf16[24,2048]{1,0:T(8,128)(2,1)S(1)}, bf16[24,2048]{1,0:T(8,128)(2,1)}, u32[]{:S(2)}) copy-start(bf16[24,2048]{1,0:T(8,128)(2,1)} %param.6) | copy-start | bytes 294916
  147.2 27.9 %copy-start.3 = (bf16[8,4,64,512]{3,2,1,0:T(8,128)(2,1)S(1)}, bf16[8,4,64,512]{3,2,1,0:T(8,128)(2,1)}, u32[]{:S(2)}) copy-start(bf16[8,4,64,512]{3,2,1,0:T(8,128)(2,1)} %get-tuple-element.12) | copy-start | bytes 6291460

commit v6 on v5

--- a/solution.py
+++ b/solution.py
@@ -135,6 +135,67 @@
 def dp_scratch(lines, ring):
     return [
         pltpu.SemaphoreType.DMA((1 + ring + (lines - 1) * 2 * ring,)),
+        pltpu.SemaphoreType.DMA((lines * ring,)),
+    ]
+
+
+def dp_direct_peers(lines, ring):
+    me = lax.axis_index("dp")
+    z, y = me // ring, me % ring
+    out = []
+    for d in range(1, lines):
+        out += [(z + d < lines, "dp", me + d * ring), (z - d >= 0, "dp", me - d * ring)]
+    return out + [(None, "dp", z * ring + (y + k) % ring) for k in range(1, ring)]
+
+
+def dp_direct_body(lines, ring, ins, outs, scratch):
+    (x_ref,), (o_ref,), (send_sem, recv_sem) = ins, outs, scratch
+    me = lax.axis_index("dp")
+    z, y = me // ring, me % ring
+    sends = []
+
+    def send(cond, src, src_z, peer):
+        slot = src_z * ring + y
+        copy = _remote(src, o_ref.at[src_z, y], send_sem.at[len(sends)], recv_sem.at[slot], "dp", peer)
+        pl.when(cond)(copy.start)
+        sends.append((cond, copy))
+
+    def spread(cond, src, src_z):
+        for k in range(1, ring):
+            send(cond, src, src_z, z * ring + (y + k) % ring)
+
+    def arrive(cond, src_z, peer):
+        slot = src_z * ring + y
+        copy = _remote(o_ref.at[src_z, y], o_ref.at[src_z, y], send_sem.at[0], recv_sem.at[slot], "dp", peer)
+        pl.when(cond)(copy.wait_recv)
+
+    always = z >= 0
+    spread(always, x_ref, z)
+    for d in range(1, lines):
+        send(z + d < lines, x_ref, z, me + d * ring)
+        send(z - d >= 0, x_ref, z, me - d * ring)
+    o_ref[z, y] = x_ref[...]
+    yield
+    for d in range(1, lines):
+        for sign in (1, -1):
+            cond = (z + sign * d < lines) & (z + sign * d >= 0)
+            src_z = jnp.clip(z + sign * d, 0, lines - 1)
+            arrive(cond, src_z, src_z * ring + y)
+            spread(cond, o_ref.at[src_z, y], src_z)
+        yield
+    for k in range(1, ring):
+        yy = (y + k) % ring
+        for zz in range(lines):
+            slot = zz * ring + yy
+            copy = _remote(o_ref.at[zz, yy], o_ref.at[zz, yy], send_sem.at[0], recv_sem.at[slot], "dp", z * ring + yy)
+            copy.wait_recv()
+    for cond, copy in sends:
+        pl.when(cond)(copy.wait_send)
+
+
+def dp_direct_scratch(lines, ring):
+    return [
+        pltpu.SemaphoreType.DMA((ring - 1 + 2 * (lines - 1) * ring,)),
         pltpu.SemaphoreType.DMA((lines * ring,)),
     ]
 
@@ -346,10 +407,10 @@
     qkv_piece = qkv_blk.reshape(mp_count * rows_w, -1)
     up_piece = up_blk.reshape(mp_count * rows_w, -1)
     (qkv_w,) = combined(
-        [(functools.partial(dp_peers, lines, RING), functools.partial(dp_gather_body, lines, RING), 1, 1, 2)],
+        [(functools.partial(dp_direct_peers, lines, RING), functools.partial(dp_direct_body, lines, RING), 1, 1, 2)],
         [qkv_piece],
         [sd((lines, RING) + qkv_piece.shape, bf)],
-        dp_scratch(lines, RING),
+        dp_direct_scratch(lines, RING),
         1,
     )
     qkv_w = qkv_w.reshape(-1, qkv_piece.shape[-1])
@@ -358,11 +419,11 @@
     share, up_w = combined(
         [
             (functools.partial(mp_peers, chips), functools.partial(mp_sum_body, chips), 1, 1, 8),
-            (functools.partial(dp_peers, lines, RING), functools.partial(dp_gather_body, lines, RING), 1, 1, 2),
+            (functools.partial(dp_direct_peers, lines, RING), functools.partial(dp_direct_body, lines, RING), 1, 1, 2),
         ],
         [partial.reshape(2, chips, 2, rows, -1), up_piece],
         [sd((rows, partial.shape[-1]), jnp.float32), sd((lines, RING) + up_piece.shape, bf)],
-        mp_sum_scratch(chips, rows, partial.shape[-1], bf) + dp_scratch(lines, RING),
+        mp_sum_scratch(chips, rows, partial.shape[-1], bf) + dp_direct_scratch(lines, RING),
         2,
     )
     up_w = up_w.reshape(-1, up_piece.shape[-1])

time: 179 us -> 184 us (1.028)
  Pallas kernels: 153 us -> 158 us
    pallas_call x4, Pallas kernels: 153 us -> 158 us  [combined(): pl.pallas_call(functools.partial(combined_kernel, parts), out_shape=out_s...]
where the time goes in v6:
time: 184 us
  Pallas kernels  158 us (86%)
  other arithmetic  12.4 us (7%)
  matrix products  8.11 us (4%)
  local copies, waits for them, and re-layouts  4.21 us (2%)
    pallas_call x4, Pallas kernels, combined(): pl.pallas_call(functools.partial(combined_kernel, parts), out_shape=out_s...  158 us

profile of v6, /device:TPU:1, one launch (start us, length us, event | category | flops | bytes accessed | tf_op | source)
XLA Modules:
  0.0 183.8 jit_solution(12818294458950097062)
XLA Ops:
  0.6 0.0 copy-start
  0.7 0.7 fusion.26
  1.4 1.0 convert_reduce_fusion
  2.4 1.1 fusion.19
  3.5 0.7 reduce.4
  4.2 1.5 convert_element_type.51
  5.8 1.6 convert_element_type.52
  7.3 1.6 fusion.20.refs_2_
  8.9 34.9 %shard_map.85 = (bf16[16,4,384]{2,1,0:T(4,128)(2,1)}, bf16[16,4,512]{2,1,0:T(4,128)(2,1)}, bf16[2,4,2,24,2048]{4,3,2,1,0:T(8,128)(2,1)}) custom-call(bf16[16,4,384]{2,1,0:T(4,128)(2,1)} %bitcast.60, bf16[16,4,512]{2,1,0:T(4,128)(2,1)} %bitcast.59, bf16[24,2048]{1,0:T(8,128)(2,1)} %fusion.20.refs_2_), custom_call_target="tpu_custom_call" | custom-call | tf_op jit(solution)/shard_map/pallas_call | solution.py:339
  43.9 0.0 copy-start.4
  43.9 1.6 reshape.143.refs_0_
  45.5 1.5 reshape.151.refs_1_
  47.0 46.9 %shard_map.86 = bf16[8,4,64,384]{3,2,1,0:T(8,128)(2,1)} custom-call(bf16[64,384]{1,0:T(8,128)(2,1)} %reshape.143.refs_0_), custom_call_target="tpu_custom_call" | custom-call | tf_op jit(solution)/shard_map/pallas_call | solution.py:339
  93.9 0.0 copy-done.4
  93.9 2.5 %convolution_convert_fusion.1 = bf16[384,384]{0,1:T(8,128)(2,1)S(1)} fusion(bf16[384,2048]{1,0:T(8,128)(2,1)S(1)} %bitcast.65, bf16[2048,384]{1,0:T(8,128)(2,1)} %bitcast.55), kind=kOutput, calls=%fused_computation.5 | convolution fusion | flops 604127232 | bytes 3440640 | tf_op jit(solution)/shard_map/dot_general | solution.py:352
  96.4 0.1 copy.15
  96.5 0.1 copy.14
  96.8 0.8 scatter_fusion
  97.6 0.0 copy-start.2
  97.6 0.4 fusion.31
  98.0 0.1 fusion.12
  98.1 0.0 copy-done
  98.1 2.0 %convolution_convert_fusion = bf16[384,2048]{1,0:T(8,128)(2,1)} fusion(bf16[128,2048]{1,0:T(8,128)(2,1)S(1)} %copy-done, f32[384,384]{0,1:T(8,128)S(1)} %get-tuple-element.24, f32[384]{0:T(512)S(1)} %fusion.12, f32[384]{0:T(512)S(1)} %get-tuple-element.23, bf16[384,1,3,128]{0,3,2,1:T(8,128)(2,1)S(1)} %bitcast.63), kind=kOutput, calls=%fused_computation.1 | convolution fusion | flops 240353280 | bytes 2789376 | tf_op jit(solution)/shard_map/dot_general | solution.py:418
  100.1 0.0 copy-done.2
  100.1 48.1 %shard_map.87 = (f32[24,2048]{1,0:T(8,128)}, bf16[8,4,64,512]{3,2,1,0:T(8,128)(2,1)}) custom-call(bf16[2,4,2,24,2048]{4,3,2,1,0:T(8,128)(2,1)} %bitcast.54, bf16[64,512]{1,0:T(8,128)(2,1)} %reshape.151.refs_1_), custom_call_target="tpu_custom_call" | custom-call | tf_op jit(solution)/shard_map/pallas_call | solution.py:339
  148.2 0.0 copy-start.3
  148.2 0.0 copy-done.1
  148.2 1.2 fusion.24
  149.4 1.1 multiply_reduce_fusion
  150.6 1.7 multiply_convert_fusion
  152.2 28.3 %shard_map.88 = bf16[2,4,2,24,2048]{4,3,2,1,0:T(8,128)(2,1)} custom-call(bf16[24,2048]{1,0:T(8,128)(2,1)} %get-tuple-element.21.refs_0_), custom_call_target="tpu_custom_call" | custom-call | tf_op jit(solution)/shard_map/pallas_call | solution.py:339
  180.5 3.3 %fusion.10 = bf16[384,512]{1,0:T(8,128)(2,1)} fusion(bf16[384,2048]{1,0:T(8,128)(2,1)} %bitcast.56, bf16[2048,512]{1,0:T(8,128)(2,1)S(1)} %bitcast.64), kind=kOutput, calls=%fused_computation.16 | convolution fusion | flops 807075840 | bytes 4063232 | tf_op jit(solution)/shard_map/dot_general | solution.py:440
  (10 shorter events, 0.1 us)
Async XLA Ops:
  0.6 97.5 %copy-start = (bf16[128,2048]{1,0:T(8,128)(2,1)S(1)}, bf16[128,2048]{1,0:T(8,128)(2,1)}, u32[]{:S(2)}) copy-start(bf16[128,2048]{1,0:T(8,128)(2,1)} %param.11) | copy-start | bytes 1572868
  43.9 50.0 %copy-start.4 = (bf16[2,4,2,24,2048]{4,3,2,1,0:T(8,128)(2,1)S(1)}, bf16[2,4,2,24,2048]{4,3,2,1,0:T(8,128)(2,1)}, u32[]{:S(2)}) copy-start(bf16[2,4,2,24,2048]{4,3,2,1,0:T(8,128)(2,1)} %get-tuple-element.8) | copy-start | bytes 4718596
  97.6 2.5 %copy-start.2 = (bf16[3,2,128,128]{3,2,1,0:T(8,128)(2,1)}, bf16[3,2,128,128]{3,2,1,0:T(8,128)(2,1)S(1)}, u32[]{:S(2)}) copy-start(bf16[3,2,128,128]{3,2,1,0:T(8,128)(2,1)S(1)} %scatter_fusion) | copy-start | bytes 589828
  100.1 48.1 %copy-start.1 = (bf16[24,2048]{1,0:T(8,128)(2,1)S(1)}, bf16[24,2048]{1,0:T(8,128)(2,1)}, u32[]{:S(2)}) copy-start(bf16[24,2048]{1,0:T(8,128)(2,1)} %param.6) | copy-start | bytes 294916
  148.2 32.3 %copy-start.3 = (bf16[8,4,64,512]{3,2,1,0:T(8,128)(2,1)S(1)}, bf16[8,4,64,512]{3,2,1,0:T(8,128)(2,1)}, u32[]{:S(2)}) copy-start(bf16[8,4,64,512]{3,2,1,0:T(8,128)(2,1)} %get-tuple-element.12) | copy-start | bytes 6291460

commit v7 on v6

--- a/solution.py
+++ b/solution.py
@@ -389,41 +389,43 @@
     up_t = up_master.astype(bf).reshape(rows_w, mp_count, -1).transpose(1, 0, 2)
     normed_own = layer_norm(hidden_in.astype(jnp.float32)).astype(bf)
     sd = jax.ShapeDtypeStruct
-    qkv_blk, up_blk, normed = combined(
+    qkv_blk, up_blk = combined(
         [
             (
                 functools.partial(exchange_peers, mp_count, "mp"),
                 functools.partial(exchange_body, mp_count, "mp"),
                 2, 2, 3,
             ),
+        ],
+        [qkv_t, up_t],
+        [sd(qkv_t.shape, bf), sd(up_t.shape, bf)],
+        exchange_scratch(mp_count, 2),
+        0,
+    )
+    qkv_piece = qkv_blk.reshape(mp_count * rows_w, -1)
+    up_piece = up_blk.reshape(mp_count * rows_w, -1)
+    qkv_w, normed = combined(
+        [
+            (functools.partial(dp_peers, lines, RING), functools.partial(dp_gather_body, lines, RING), 1, 1, 2),
             (functools.partial(mp_peers, chips), functools.partial(mp_gather_body, chips), 1, 1, 2),
         ],
-        [qkv_t, up_t, normed_own],
-        [sd(qkv_t.shape, bf), sd(up_t.shape, bf), sd((2, chips, 2) + normed_own.shape, bf)],
-        exchange_scratch(mp_count, 2) + mp_gather_scratch(chips),
-        0,
+        [qkv_piece, normed_own],
+        [sd((lines, RING) + qkv_piece.shape, bf), sd((2, chips, 2) + normed_own.shape, bf)],
+        dp_scratch(lines, RING) + mp_gather_scratch(chips),
+        1,
     )
     normed = normed.reshape(mp_count * rows, -1)
-    qkv_piece = qkv_blk.reshape(mp_count * rows_w, -1)
-    up_piece = up_blk.reshape(mp_count * rows_w, -1)
-    (qkv_w,) = combined(
-        [(functools.partial(dp_direct_peers, lines, RING), functools.partial(dp_direct_body, lines, RING), 1, 1, 2)],
-        [qkv_piece],
-        [sd((lines, RING) + qkv_piece.shape, bf)],
-        dp_direct_scratch(lines, RING),
-        1,
-    )
     qkv_w = qkv_w.reshape(-1, qkv_piece.shape[-1])
     context, cache = attend(normed, qkv_w, segment_ids[0], page_table[0], mp_index)
     partial = jnp.dot(context, dense_weight, preferred_element_type=jnp.float32).astype(bf)
     share, up_w = combined(
         [
             (functools.partial(mp_peers, chips), functools.partial(mp_sum_body, chips), 1, 1, 8),
-            (functools.partial(dp_direct_peers, lines, RING), functools.partial(dp_direct_body, lines, RING), 1, 1, 2),
+            (functools.partial(dp_peers, lines, RING), functools.partial(dp_gather_body, lines, RING), 1, 1, 2),
         ],
         [partial.reshape(2, chips, 2, rows, -1), up_piece],
         [sd((rows, partial.shape[-1]), jnp.float32), sd((lines, RING) + up_piece.shape, bf)],
-        mp_sum_scratch(chips, rows, partial.shape[-1], bf) + dp_direct_scratch(lines, RING),
+        mp_sum_scratch(chips, rows, partial.shape[-1], bf) + dp_scratch(lines, RING),
         2,
     )
     up_w = up_w.reshape(-1, up_piece.shape[-1])

time: 184 us -> 176 us (0.957)
  Pallas kernels: 158 us -> 149 us
    pallas_call x4, Pallas kernels: 158 us -> 149 us  [combined(): pl.pallas_call(functools.partial(combined_kernel, parts), out_shape=out_s...]
where the time goes in v7:
time: 176 us; the launch traced here: 175 us
  Pallas kernels  149 us (85%)
  other arithmetic  12.4 us (7%)
  matrix products  8.54 us (5%)
  local copies, waits for them, and re-layouts  4.08 us (2%)
    pallas_call x4, Pallas kernels, combined(): pl.pallas_call(functools.partial(combined_kernel, parts), out_shape=out_s...  149 us

profile of v7, /device:TPU:1, one launch (start us, length us, event | category | flops | bytes accessed | tf_op | source)
XLA Modules:
  0.0 175.0 jit_solution(6176361576830566190)
XLA Ops:
  0.6 0.0 copy-start
  0.7 0.7 fusion.26
  1.4 1.0 convert_reduce_fusion
  2.4 1.1 fusion.19
  3.5 0.7 reduce.4
  4.2 1.5 convert_element_type.51
  5.8 1.6 convert_element_type.52
  7.3 24.3 %shard_map.85 = (bf16[16,4,384]{2,1,0:T(4,128)(2,1)}, bf16[16,4,512]{2,1,0:T(4,128)(2,1)}) custom-call(bf16[16,4,384]{2,1,0:T(4,128)(2,1)} %bitcast.59, bf16[16,4,512]{2,1,0:T(4,128)(2,1)} %bitcast.58), custom_call_target="tpu_custom_call" | custom-call | tf_op jit(solution)/shard_map/pallas_call | solution.py:339
  31.7 1.4 reshape.142.refs_0_
  33.1 1.5 reshape.151.refs_1_
  34.6 1.6 fusion.20.refs_1_
  36.2 47.2 %shard_map.86 = (bf16[8,4,64,384]{3,2,1,0:T(8,128)(2,1)}, bf16[2,4,2,24,2048]{4,3,2,1,0:T(8,128)(2,1)}) custom-call(bf16[64,384]{1,0:T(8,128)(2,1)} %reshape.142.refs_0_, bf16[24,2048]{1,0:T(8,128)(2,1)} %fusion.20.refs_1_), custom_call_target="tpu_custom_call" | custom-call | tf_op jit(solution)/shard_map/pallas_call | solution.py:339
  83.4 2.9 %convolution_convert_fusion.1 = bf16[384,384]{0,1:T(8,128)(2,1)S(1)} fusion(bf16[384,2048]{1,0:T(8,128)(2,1)} %bitcast.65, bf16[2048,384]{1,0:T(8,128)(2,1)} %bitcast.64), kind=kOutput, calls=%fused_computation.5 | convolution fusion | flops 604127232 | bytes 3440640 | tf_op jit(solution)/shard_map/dot_general | solution.py:352
  86.4 0.1 copy.15
  86.5 0.1 copy.14
  86.7 0.8 scatter_fusion
  87.6 0.0 copy-start.2
  87.6 0.4 fusion.31
  88.0 0.1 fusion.12
  88.1 0.0 copy-done
  88.1 2.0 %convolution_convert_fusion = bf16[384,2048]{1,0:T(8,128)(2,1)} fusion(bf16[128,2048]{1,0:T(8,128)(2,1)S(1)} %copy-done, f32[384,384]{0,1:T(8,128)S(1)} %get-tuple-element.26, f32[384]{0:T(512)S(1)} %fusion.12, f32[384]{0:T(512)S(1)} %get-tuple-element.25, bf16[384,1,3,128]{0,3,2,1:T(8,128)(2,1)S(1)} %bitcast.62), kind=kOutput, calls=%fused_computation.1 | convolution fusion | flops 240353280 | bytes 2789376 | tf_op jit(solution)/shard_map/dot_general | solution.py:420
  90.1 0.0 copy-done.2
  90.1 0.0 copy-start.1
  90.1 53.3 %shard_map.87 = (f32[24,2048]{1,0:T(8,128)}, bf16[8,4,64,512]{3,2,1,0:T(8,128)(2,1)}) custom-call(bf16[2,4,2,24,2048]{4,3,2,1,0:T(8,128)(2,1)} %bitcast.54, bf16[64,512]{1,0:T(8,128)(2,1)} %reshape.151.refs_1_), custom_call_target="tpu_custom_call" | custom-call | tf_op jit(solution)/shard_map/pallas_call | solution.py:339
  143.4 0.0 copy-start.3
  143.4 0.0 copy-done.1
  143.4 1.2 fusion.24
  144.6 1.1 multiply_reduce_fusion
  145.7 1.7 multiply_convert_fusion
  147.4 24.3 %shard_map.88 = bf16[2,4,2,24,2048]{4,3,2,1,0:T(8,128)(2,1)} custom-call(bf16[24,2048]{1,0:T(8,128)(2,1)} %get-tuple-element.23.refs_0_), custom_call_target="tpu_custom_call" | custom-call | tf_op jit(solution)/shard_map/pallas_call | solution.py:339
  171.7 0.0 copy-done.3
  171.7 3.3 %fusion.10 = bf16[384,512]{1,0:T(8,128)(2,1)} fusion(bf16[384,2048]{1,0:T(8,128)(2,1)} %bitcast.55, bf16[2048,512]{1,0:T(8,128)(2,1)S(1)} %bitcast.63), kind=kOutput, calls=%fused_computation.16 | convolution fusion | flops 807075840 | bytes 4063232 | tf_op jit(solution)/shard_map/dot_general | solution.py:442
  (8 shorter events, 0.1 us)
Async XLA Ops:
  0.6 87.5 %copy-start = (bf16[128,2048]{1,0:T(8,128)(2,1)S(1)}, bf16[128,2048]{1,0:T(8,128)(2,1)}, u32[]{:S(2)}) copy-start(bf16[128,2048]{1,0:T(8,128)(2,1)} %param.11) | copy-start | bytes 1572868
  87.6 2.5 %copy-start.2 = (bf16[3,2,128,128]{3,2,1,0:T(8,128)(2,1)}, bf16[3,2,128,128]{3,2,1,0:T(8,128)(2,1)S(1)}, u32[]{:S(2)}) copy-start(bf16[3,2,128,128]{3,2,1,0:T(8,128)(2,1)S(1)} %scatter_fusion) | copy-start | bytes 589828
  90.1 53.3 %copy-start.1 = (bf16[24,2048]{1,0:T(8,128)(2,1)S(1)}, bf16[24,2048]{1,0:T(8,128)(2,1)}, u32[]{:S(2)}) copy-start(bf16[24,2048]{1,0:T(8,128)(2,1)} %param.6) | copy-start | bytes 294916
  143.4 28.4 %copy-start.3 = (bf16[8,4,64,512]{3,2,1,0:T(8,128)(2,1)S(1)}, bf16[8,4,64,512]{3,2,1,0:T(8,128)(2,1)}, u32[]{:S(2)}) copy-start(bf16[8,4,64,512]{3,2,1,0:T(8,128)(2,1)} %get-tuple-element.14) | copy-start | bytes 6291460

commit v8 on v7

--- a/solution.py
+++ b/solution.py
@@ -198,6 +198,72 @@
         pltpu.SemaphoreType.DMA((ring - 1 + 2 * (lines - 1) * ring,)),
         pltpu.SemaphoreType.DMA((lines * ring,)),
     ]
+
+
+def dp_yfirst_body(lines, ring, ins, outs, scratch):
+    (x_ref,), (o_ref,), (send_sem, recv_sem, local_sem) = ins, outs, scratch
+    me = lax.axis_index("dp")
+    z, y = me // ring, me % ring
+    has_left, has_right = z > 0, z < lines - 1
+    sends = []
+
+    def send(cond, src, dst, slot, peer):
+        copy = _remote(src, dst, send_sem.at[len(sends)], recv_sem.at[slot], "dp", peer)
+        pl.when(cond)(copy.start)
+        sends.append((cond, copy))
+
+    def arrive(cond, dst, slot, peer):
+        copy = _remote(dst, dst, send_sem.at[0], recv_sem.at[slot], "dp", peer)
+        pl.when(cond)(copy.wait_recv)
+
+    always = z >= 0
+    for k in range(1, ring):
+        send(always, x_ref, o_ref.at[z, y], lines + y, z * ring + (y + k) % ring)
+    own = pltpu.make_async_copy(x_ref, o_ref.at[z, y], local_sem.at[0])
+    own.start()
+    yield
+    for k in range(1, ring):
+        yy = (y + k) % ring
+        arrive(always, o_ref.at[z, yy], lines + yy, z * ring + yy)
+    own.wait()
+    send(has_right, o_ref.at[z], o_ref.at[z], z, me + ring)
+    send(has_left, o_ref.at[z], o_ref.at[z], z, me - ring)
+    yield
+    for s in range(1, lines):
+        from_left = z - s >= 0
+        src_l = jnp.maximum(z - s, 0)
+        arrive(from_left, o_ref.at[src_l], src_l, me - ring)
+        send(from_left & has_right, o_ref.at[src_l], o_ref.at[src_l], src_l, me + ring)
+        from_right = z + s <= lines - 1
+        src_r = jnp.minimum(z + s, lines - 1)
+        arrive(from_right, o_ref.at[src_r], src_r, me + ring)
+        send(from_right & has_left, o_ref.at[src_r], o_ref.at[src_r], src_r, me - ring)
+        yield
+    for cond, copy in sends:
+        pl.when(cond)(copy.wait_send)
+
+
+def dp_yfirst_scratch(lines, ring):
+    return [
+        pltpu.SemaphoreType.DMA((ring - 1 + 2 * lines,)),
+        pltpu.SemaphoreType.DMA((lines + ring,)),
+        pltpu.SemaphoreType.DMA((1,)),
+    ]
+
+
+def dp_split_parts(lines, ring):
+    return [
+        (functools.partial(dp_peers, lines, ring), functools.partial(dp_gather_body, lines, ring), 1, 1, 2),
+        (functools.partial(dp_peers, lines, ring), functools.partial(dp_yfirst_body, lines, ring), 1, 1, 3),
+    ]
+
+
+def dp_split_scratch(lines, ring):
+    return dp_scratch(lines, ring) + dp_yfirst_scratch(lines, ring)
+
+
+def dp_split_join(first, second):
+    return jnp.concatenate([first, second], axis=2).reshape(-1, first.shape[-1])
 
 
 def mp_peers(chips):
@@ -404,31 +470,36 @@
     )
     qkv_piece = qkv_blk.reshape(mp_count * rows_w, -1)
     up_piece = up_blk.reshape(mp_count * rows_w, -1)
-    qkv_w, normed = combined(
+    half = qkv_piece.shape[0] // 2
+    qkv_a, qkv_b, normed = combined(
+        dp_split_parts(lines, RING)
+        + [(functools.partial(mp_peers, chips), functools.partial(mp_gather_body, chips), 1, 1, 2)],
+        [qkv_piece[:half], qkv_piece[half:], normed_own],
         [
-            (functools.partial(dp_peers, lines, RING), functools.partial(dp_gather_body, lines, RING), 1, 1, 2),
-            (functools.partial(mp_peers, chips), functools.partial(mp_gather_body, chips), 1, 1, 2),
+            sd((lines, RING, half, qkv_piece.shape[-1]), bf),
+            sd((lines, RING, half, qkv_piece.shape[-1]), bf),
+            sd((2, chips, 2) + normed_own.shape, bf),
         ],
-        [qkv_piece, normed_own],
-        [sd((lines, RING) + qkv_piece.shape, bf), sd((2, chips, 2) + normed_own.shape, bf)],
-        dp_scratch(lines, RING) + mp_gather_scratch(chips),
+        dp_split_scratch(lines, RING) + mp_gather_scratch(chips),
         1,
     )
     normed = normed.reshape(mp_count * rows, -1)
-    qkv_w = qkv_w.reshape(-1, qkv_piece.shape[-1])
+    qkv_w = dp_split_join(qkv_a, qkv_b)
     context, cache = attend(normed, qkv_w, segment_ids[0], page_table[0], mp_index)
     partial = jnp.dot(context, dense_weight, preferred_element_type=jnp.float32).astype(bf)
-    share, up_w = combined(
+    share, up_a, up_b = combined(
+        [(functools.partial(mp_peers, chips), functools.partial(mp_sum_body, chips), 1, 1, 8)]
+        + dp_split_parts(lines, RING),
+        [partial.reshape(2, chips, 2, rows, -1), up_piece[:half], up_piece[half:]],
         [
-            (functools.partial(mp_peers, chips), functools.partial(mp_sum_body, chips), 1, 1, 8),
-            (functools.partial(dp_peers, lines, RING), functools.partial(dp_gather_body, lines, RING), 1, 1, 2),
+            sd((rows, partial.shape[-1]), jnp.float32),
+            sd((lines, RING, half, up_piece.shape[-1]), bf),
+            sd((lines, RING, half, up_piece.shape[-1]), bf),
         ],
-        [partial.reshape(2, chips, 2, rows, -1), up_piece],
-        [sd((rows, partial.shape[-1]), jnp.float32), sd((lines, RING) + up_piece.shape, bf)],
-        mp_sum_scratch(chips, rows, partial.shape[-1], bf) + dp_scratch(lines, RING),
+        mp_sum_scratch(chips, rows, partial.shape[-1], bf) + dp_split_scratch(lines, RING),
         2,
     )
-    up_w = up_w.reshape(-1, up_piece.shape[-1])
+    up_w = dp_split_join(up_a, up_b)
     stream_own = hidden_in.astype(jnp.float32) + share
     normed_two_own = layer_norm(stream_own).astype(bf)
     (normed_two,) = combined(

time: 176 us -> 181 us (1.028)
  Pallas kernels: 149 us -> 156 us
  matrix products: 8.54 us -> 6.67 us
    pallas_call x4, Pallas kernels: 149 us -> 156 us  [combined(): pl.pallas_call(functools.partial(combined_kernel, parts), out_shape=out_s...]
    concatenate x0 -> x2, other arithmetic: none -> 3.48 us  [dp_split_join(): return jnp.concatenate([first, second], axis=2).reshape(-1, first.shape[-1])]
    slice x0 -> x6, local copies, waits for them, and re-layouts: none -> 3.3 us  [the longest x2 1.4 us: local(): qkv_piece[half:]]
    reshape x2 -> x0, local copies, waits for them, and re-layouts: 2.92 us -> none  [the longest x1 1.49 us: local(): up_piece = up_blk.reshape(mp_count * rows_w, -1)]
    dot_general x1, matrix products: 2.91 us -> 1.04 us  [attend(): jnp.dot(normed, qkv_w, preferred_element_type=jnp.float32)]
where the time goes in v8:
time: 181 us; the launch traced here: 180 us
  Pallas kernels  156 us (86%)
  other arithmetic  11.6 us (6%)
  matrix products  6.67 us (4%)
  local copies, waits for them, and re-layouts  5.59 us (3%)
    pallas_call x4, Pallas kernels, combined(): pl.pallas_call(functools.partial(combined_kernel, parts), out_shape=out_s...  156 us

profile of v8, /device:TPU:1, one launch (start us, length us, event | category | flops | bytes accessed | tf_op | source)
XLA Modules:
  0.0 180.4 jit_solution(7218273598262611838)
XLA Ops:
  0.6 0.0 copy-start
  0.6 1.6 convert_element_type.52
  2.3 1.5 convert_element_type.51
  3.8 24.3 %shard_map.85 = (bf16[16,4,384]{2,1,0:T(4,128)(2,1)}, bf16[16,4,512]{2,1,0:T(4,128)(2,1)}) custom-call(bf16[16,4,384]{2,1,0:T(4,128)(2,1)} %bitcast.60, bf16[16,4,512]{2,1,0:T(4,128)(2,1)} %bitcast.59), custom_call_target="tpu_custom_call" | custom-call | tf_op jit(solution)/shard_map/pallas_call | solution.py:405
  28.1 0.8 fusion.32
  28.9 0.6 slice.34.refs_0_
  29.5 0.6 slice.36.refs_1_
  30.1 1.0 convert_reduce_fusion
  31.2 1.1 fusion.19
  32.3 1.6 fusion.20.refs_2_
  33.9 47.8 %shard_map.86 = (bf16[8,4,32,384]{3,2,1,0:T(8,128)(2,1)}, bf16[8,4,32,384]{3,2,1,0:T(8,128)(2,1)}, bf16[2,4,2,24,2048]{4,3,2,1,0:T(8,128)(2,1)}) custom-call(bf16[32,384]{1,0:T(8,128)(2,1)} %slice.34.refs_0_, bf16[32,384]{1,0:T(8,128)(2,1)} %slice.36.refs_1_, bf16[24,2048]{1,0:T(8,128)(2,1)} %fusion.20.refs_2_), custom_call_target="tpu_custom_call" | custom-call | tf_op jit(solution)/shard_map/pallas_call | solution.py:405
  81.7 1.7 pad_maximum_fusion.1
  83.5 0.1 copy-done.6
  83.6 1.0 convolution_convert_fusion.1
  84.7 0.4 fusion.33
  85.1 0.1 fusion.12
  85.3 2.0 %convolution_convert_fusion = bf16[384,2048]{1,0:T(8,128)(2,1)} fusion(bf16[128,2048]{1,0:T(8,128)(2,1)S(1)} %copy-done, f32[384,384]{0,1:T(8,128)S(1)} %get-tuple-element.34, f32[384]{0:T(512)S(1)} %fusion.12, f32[384]{0:T(512)S(1)} %get-tuple-element.33, bf16[384,1,3,128]{0,3,2,1:T(8,128)(2,1)S(1)} %bitcast.62), kind=kOutput, calls=%fused_computation.1 | convolution fusion | flops 240353280 | bytes 2789376 | tf_op jit(solution)/shard_map/dot_general | solution.py:489
  87.3 0.6 slice.41.refs_1_
  87.9 0.6 slice.43.refs_2_
  88.5 56.8 %shard_map.87 = (f32[24,2048]{1,0:T(8,128)}, bf16[8,4,32,512]{3,2,1,0:T(8,128)(2,1)}, bf16[8,4,32,512]{3,2,1,0:T(8,128)(2,1)}) custom-call(bf16[2,4,2,24,2048]{4,3,2,1,0:T(8,128)(2,1)} %bitcast.54, bf16[32,512]{1,0:T(8,128)(2,1)} %slice.41.refs_1_, bf16[32,512]{1,0:T(8,128)(2,1)} %slice.43.refs_2_), custom_call_target="tpu_custom_call" | custom-call | tf_op jit(solution)/shard_map/pallas_call | solution.py:405
  145.3 0.0 copy-start.1
  145.3 1.7 pad_maximum_fusion
  147.1 0.1 fusion.24
  147.3 0.2 multiply_reduce_fusion
  147.5 0.7 multiply_convert_fusion
  148.2 26.6 %shard_map.88 = bf16[2,4,2,24,2048]{4,3,2,1,0:T(8,128)(2,1)} custom-call(bf16[24,2048]{1,0:T(8,128)(2,1)} %get-tuple-element.27.refs_0_), custom_call_target="tpu_custom_call" | custom-call | tf_op jit(solution)/shard_map/pallas_call | solution.py:405
  174.9 3.3 %fusion.10 = bf16[384,512]{1,0:T(8,128)(2,1)} fusion(bf16[384,2048]{1,0:T(8,128)(2,1)} %bitcast.56, bf16[2048,512]{1,0:T(8,128)(2,1)S(1)} %bitcast.53), kind=kOutput, calls=%fused_computation.18 | convolution fusion | flops 807075840 | bytes 4063232 | tf_op jit(solution)/shard_map/dot_general | solution.py:513
  178.2 0.1 copy.14
  178.3 0.1 copy.15
  178.5 0.3 copy-done.7
  178.8 0.8 scatter_fusion
  179.7 0.7 copy-done.3
  (22 shorter events, 0.2 us)
Async XLA Ops:
  0.6 84.6 %copy-start = (bf16[128,2048]{1,0:T(8,128)(2,1)S(1)}, bf16[128,2048]{1,0:T(8,128)(2,1)}, u32[]{:S(2)}) copy-start(bf16[128,2048]{1,0:T(8,128)(2,1)} %param.11) | copy-start | bytes 1572868
  81.7 1.9 %copy-start.6 = (bf16[2,4,2,24,2048]{4,3,2,1,0:T(8,128)(2,1)S(1)}, bf16[2,4,2,24,2048]{4,3,2,1,0:T(8,128)(2,1)}, u32[]{:S(2)}) copy-start(bf16[2,4,2,24,2048]{4,3,2,1,0:T(8,128)(2,1)} %get-tuple-element.12) | copy-start | bytes 4718596
  83.6 1.1 copy-start.5
  85.3 2.0 %copy-start.4 = (bf16[16,4,512]{2,1,0:T(4,128)(2,1)S(1)}, bf16[16,4,512]{2,1,0:T(4,128)(2,1)}, u32[]{:S(2)}) copy-start(bf16[16,4,512]{2,1,0:T(4,128)(2,1)} %get-tuple-element.15) | copy-start | bytes 196612
  145.3 1.8 copy-start.1
  145.3 1.8 copy-start.2
  178.1 0.7 copy-start.7
  179.7 0.7 copy-start.3

commit v9 on v7

--- a/solution.py
+++ b/solution.py
@@ -198,6 +198,20 @@
         pltpu.SemaphoreType.DMA((ring - 1 + 2 * (lines - 1) * ring,)),
         pltpu.SemaphoreType.DMA((lines * ring,)),
     ]
+
+
+def weights_peers(n, lines, ring):
+    return exchange_peers(n, "mp") + dp_peers(lines, ring)
+
+
+def weights_body(n, lines, ring, ins, outs, scratch):
+    (qkv_t, up_t), (qkv_full, up_blk) = ins, outs
+    ex_send, ex_recv, ex_local, qkv_blk, qkv_rows, dp_send, dp_recv = scratch
+    yield from exchange_body(n, "mp", [qkv_t, up_t], [qkv_blk, up_blk], (ex_send, ex_recv, ex_local))
+    per = qkv_blk.shape[1]
+    for m in range(n):
+        qkv_rows[m * per:(m + 1) * per, :] = qkv_blk[m]
+    yield from dp_gather_body(lines, ring, [qkv_rows], [qkv_full], (dp_send, dp_recv))
 
 
 def mp_peers(chips):
@@ -389,33 +403,31 @@
     up_t = up_master.astype(bf).reshape(rows_w, mp_count, -1).transpose(1, 0, 2)
     normed_own = layer_norm(hidden_in.astype(jnp.float32)).astype(bf)
     sd = jax.ShapeDtypeStruct
-    qkv_blk, up_blk = combined(
+    qkv_rows = sd((mp_count * rows_w, qkv_t.shape[-1]), bf)
+    qkv_w, up_blk, normed = combined(
         [
             (
-                functools.partial(exchange_peers, mp_count, "mp"),
-                functools.partial(exchange_body, mp_count, "mp"),
-                2, 2, 3,
+                functools.partial(weights_peers, mp_count, lines, RING),
+                functools.partial(weights_body, mp_count, lines, RING),
+                2, 2, 7,
             ),
-        ],
-        [qkv_t, up_t],
-        [sd(qkv_t.shape, bf), sd(up_t.shape, bf)],
-        exchange_scratch(mp_count, 2),
-        0,
-    )
-    qkv_piece = qkv_blk.reshape(mp_count * rows_w, -1)
-    up_piece = up_blk.reshape(mp_count * rows_w, -1)
-    qkv_w, normed = combined(
-        [
-            (functools.partial(dp_peers, lines, RING), functools.partial(dp_gather_body, lines, RING), 1, 1, 2),
             (functools.partial(mp_peers, chips), functools.partial(mp_gather_body, chips), 1, 1, 2),
         ],
-        [qkv_piece, normed_own],
-        [sd((lines, RING) + qkv_piece.shape, bf), sd((2, chips, 2) + normed_own.shape, bf)],
-        dp_scratch(lines, RING) + mp_gather_scratch(chips),
+        [qkv_t, up_t, normed_own],
+        [
+            sd((lines, RING) + qkv_rows.shape, bf),
+            sd(up_t.shape, bf),
+            sd((2, chips, 2) + normed_own.shape, bf),
+        ],
+        exchange_scratch(mp_count, 2)
+        + [pltpu.VMEM(qkv_t.shape, bf), pltpu.VMEM(qkv_rows.shape, bf)]
+        + dp_scratch(lines, RING)
+        + mp_gather_scratch(chips),
         1,
     )
     normed = normed.reshape(mp_count * rows, -1)
-    qkv_w = qkv_w.reshape(-1, qkv_piece.shape[-1])
+    qkv_w = qkv_w.reshape(-1, qkv_t.shape[-1])
+    up_piece = up_blk.reshape(mp_count * rows_w, -1)
     context, cache = attend(normed, qkv_w, segment_ids[0], page_table[0], mp_index)
     partial = jnp.dot(context, dense_weight, preferred_element_type=jnp.float32).astype(bf)
     share, up_w = combined(

time: 176 us -> 165 us (0.938)
  Pallas kernels: 149 us -> 141 us
  local copies, waits for them, and re-layouts: 4.08 us -> 1.81 us
    pallas_call x4 -> x3, Pallas kernels: 149 us -> 141 us  [combined(): pl.pallas_call(functools.partial(combined_kernel, parts), out_shape=out_s...]
where the time goes in v9:
time: 165 us; the launch traced here: 164 us
  Pallas kernels  141 us (85%)
  other arithmetic  12.4 us (8%)
  matrix products  8.58 us (5%)
  local copies, waits for them, and re-layouts  1.81 us (1%)
    pallas_call x3, Pallas kernels, combined(): pl.pallas_call(functools.partial(combined_kernel, parts), out_shape=out_s...  141 us

profile of v9, /device:TPU:1, one launch (start us, length us, event | category | flops | bytes accessed | tf_op | source)
XLA Modules:
  0.0 164.4 jit_solution(9589279158384081400)
XLA Ops:
  0.6 0.0 copy-start
  0.7 0.7 fusion.26
  1.4 1.0 convert_reduce_fusion
  2.4 1.1 fusion.19
  3.5 0.7 reduce.4
  4.2 1.5 convert_element_type.51
  5.8 1.6 convert_element_type.52
  7.3 1.6 fusion.20.refs_2_
  8.9 59.8 %shard_map.85 = (bf16[8,4,64,384]{3,2,1,0:T(8,128)(2,1)}, bf16[16,4,512]{2,1,0:T(4,128)(2,1)}, bf16[2,4,2,24,2048]{4,3,2,1,0:T(8,128)(2,1)}) custom-call(bf16[16,4,384]{2,1,0:T(4,128)(2,1)} %bitcast.59, bf16[16,4,512]{2,1,0:T(4,128)(2,1)} %bitcast.58, bf16[24,2048]{1,0:T(8,128)(2,1)} %fusion.20.refs_2_), custom_call_target="tpu_custom_call" | custom-call | tf_op jit(solution)/shard_map/pallas_call | solution.py:353
  68.8 0.0 copy-start.3
  68.8 2.9 %convolution_convert_fusion.1 = bf16[384,384]{0,1:T(8,128)(2,1)S(1)} fusion(bf16[384,2048]{1,0:T(8,128)(2,1)} %bitcast.65, bf16[2048,384]{1,0:T(8,128)(2,1)} %bitcast.64), kind=kOutput, calls=%fused_computation.5 | convolution fusion | flops 604127232 | bytes 3440640 | tf_op jit(solution)/shard_map/dot_general | solution.py:366
  71.7 0.0 copy-done.3
  71.7 0.6 reshape.147.refs_1_
  72.4 0.1 copy.15
  72.5 0.1 copy.14
  72.8 0.8 scatter_fusion
  73.6 0.0 copy-start.2
  73.6 0.4 fusion.31
  74.0 0.1 fusion.12
  74.1 0.0 copy-done
  74.1 2.0 %convolution_convert_fusion = bf16[384,2048]{1,0:T(8,128)(2,1)} fusion(bf16[128,2048]{1,0:T(8,128)(2,1)S(1)} %copy-done, f32[384,384]{0,1:T(8,128)S(1)} %get-tuple-element.24, f32[384]{0:T(512)S(1)} %fusion.12, f32[384]{0:T(512)S(1)} %get-tuple-element.23, bf16[384,1,3,128]{0,3,2,1:T(8,128)(2,1)S(1)} %bitcast.62), kind=kOutput, calls=%fused_computation.1 | convolution fusion | flops 240353280 | bytes 2789376 | tf_op jit(solution)/shard_map/dot_general | solution.py:432
  76.1 0.0 copy-done.2
  76.1 0.0 copy-start.1
  76.1 56.4 %shard_map.86 = (f32[24,2048]{1,0:T(8,128)}, bf16[8,4,64,512]{3,2,1,0:T(8,128)(2,1)}) custom-call(bf16[2,4,2,24,2048]{4,3,2,1,0:T(8,128)(2,1)} %bitcast.54, bf16[64,512]{1,0:T(8,128)(2,1)} %reshape.147.refs_1_), custom_call_target="tpu_custom_call" | custom-call | tf_op jit(solution)/shard_map/pallas_call | solution.py:353
  132.5 0.0 copy-start.4
  132.5 0.0 copy-done.1
  132.5 1.2 fusion.24
  133.7 1.1 multiply_reduce_fusion
  134.9 1.7 %multiply_convert_fusion = (bf16[24,2048]{1,0:T(8,128)(2,1)}, bf16[24,2048]{1,0:T(8,128)(2,1)}) fusion(f32[24]{0:T(128)S(1)} %add_rsqrt_fusion, f32[24]{0:T(128)S(1)} %broadcast_multiply_fusion, f32[24,2048]{1,0:T(8,128)} %get-tuple-element.11, bf16[24,2048]{1,0:T(8,128)(2,1)S(1)} %copy-done.1), kind=kLoop, calls=%fused_computation.33 | loop fusion | flops 294912 | bytes 491712 | tf_op jit(solution)/shard_map/convert_element_type | solution.py:445
  136.5 24.5 %shard_map.87 = bf16[2,4,2,24,2048]{4,3,2,1,0:T(8,128)(2,1)} custom-call(bf16[24,2048]{1,0:T(8,128)(2,1)} %get-tuple-element.21.refs_0_), custom_call_target="tpu_custom_call" | custom-call | tf_op jit(solution)/shard_map/pallas_call | solution.py:353
  161.1 0.0 copy-done.4
  161.1 3.3 %fusion.10 = bf16[384,512]{1,0:T(8,128)(2,1)} fusion(bf16[384,2048]{1,0:T(8,128)(2,1)} %bitcast.55, bf16[2048,512]{1,0:T(8,128)(2,1)S(1)} %bitcast.63), kind=kOutput, calls=%fused_computation.16 | convolution fusion | flops 807075840 | bytes 4063232 | tf_op jit(solution)/shard_map/dot_general | solution.py:454
  (8 shorter events, 0.1 us)
Async XLA Ops:
  0.6 73.5 %copy-start = (bf16[128,2048]{1,0:T(8,128)(2,1)S(1)}, bf16[128,2048]{1,0:T(8,128)(2,1)}, u32[]{:S(2)}) copy-start(bf16[128,2048]{1,0:T(8,128)(2,1)} %param.11) | copy-start | bytes 1572868
  68.8 3.0 %copy-start.3 = (bf16[16,4,512]{2,1,0:T(4,128)(2,1)S(1)}, bf16[16,4,512]{2,1,0:T(4,128)(2,1)}, u32[]{:S(2)}) copy-start(bf16[16,4,512]{2,1,0:T(4,128)(2,1)} %get-tuple-element.10) | copy-start | bytes 196612
  73.6 2.5 %copy-start.2 = (bf16[3,2,128,128]{3,2,1,0:T(8,128)(2,1)}, bf16[3,2,128,128]{3,2,1,0:T(8,128)(2,1)S(1)}, u32[]{:S(2)}) copy-start(bf16[3,2,128,128]{3,2,1,0:T(8,128)(2,1)S(1)} %scatter_fusion) | copy-start | bytes 589828
  76.1 56.4 %copy-start.1 = (bf16[24,2048]{1,0:T(8,128)(2,1)S(1)}, bf16[24,2048]{1,0:T(8,128)(2,1)}, u32[]{:S(2)}) copy-start(bf16[24,2048]{1,0:T(8,128)(2,1)} %param.6) | copy-start | bytes 294916
  132.5 28.6 %copy-start.4 = (bf16[8,4,64,512]{3,2,1,0:T(8,128)(2,1)S(1)}, bf16[8,4,64,512]{3,2,1,0:T(8,128)(2,1)}, u32[]{:S(2)}) copy-start(bf16[8,4,64,512]{3,2,1,0:T(8,128)(2,1)} %get-tuple-element.12) | copy-start | bytes 6291460

commit v10 on v9

--- a/solution.py
+++ b/solution.py
@@ -212,6 +212,20 @@
     for m in range(n):
         qkv_rows[m * per:(m + 1) * per, :] = qkv_blk[m]
     yield from dp_gather_body(lines, ring, [qkv_rows], [qkv_full], (dp_send, dp_recv))
+
+
+def tail_peers(chips):
+    return mp_peers(chips) + mp_peers(chips)
+
+
+def tail_body(chips, ins, outs, scratch):
+    (p_ref, h_ref), (hidden_ref, normed_ref) = ins, outs
+    sum_scratch, (share, own), gather_scratch = scratch[:8], scratch[8:10], scratch[10:]
+    yield from mp_sum_body(chips, [p_ref], [share], sum_scratch)
+    stream = h_ref[...].astype(jnp.float32) + share[...]
+    hidden_ref[...] = stream.astype(hidden_ref.dtype)
+    own[...] = layer_norm(stream).astype(own.dtype)
+    yield from mp_gather_body(chips, [own], [normed_ref], gather_scratch)
 
 
 def mp_peers(chips):
@@ -430,30 +444,29 @@
     up_piece = up_blk.reshape(mp_count * rows_w, -1)
     context, cache = attend(normed, qkv_w, segment_ids[0], page_table[0], mp_index)
     partial = jnp.dot(context, dense_weight, preferred_element_type=jnp.float32).astype(bf)
-    share, up_w = combined(
+    cols = partial.shape[-1]
+    hidden_out, normed_two, up_w = combined(
         [
-            (functools.partial(mp_peers, chips), functools.partial(mp_sum_body, chips), 1, 1, 8),
+            (functools.partial(tail_peers, chips), functools.partial(tail_body, chips), 2, 2, 12),
             (functools.partial(dp_peers, lines, RING), functools.partial(dp_gather_body, lines, RING), 1, 1, 2),
         ],
-        [partial.reshape(2, chips, 2, rows, -1), up_piece],
-        [sd((rows, partial.shape[-1]), jnp.float32), sd((lines, RING) + up_piece.shape, bf)],
-        mp_sum_scratch(chips, rows, partial.shape[-1], bf) + dp_scratch(lines, RING),
+        [partial.reshape(2, chips, 2, rows, -1), hidden_in, up_piece],
+        [
+            sd((rows, cols), bf),
+            sd((2, chips, 2, rows, cols), bf),
+            sd((lines, RING) + up_piece.shape, bf),
+        ],
+        mp_sum_scratch(chips, rows, cols, bf)
+        + [pltpu.VMEM((rows, cols), jnp.float32), pltpu.VMEM((rows, cols), bf)]
+        + mp_gather_scratch(chips)
+        + dp_scratch(lines, RING),
         2,
     )
     up_w = up_w.reshape(-1, up_piece.shape[-1])
-    stream_own = hidden_in.astype(jnp.float32) + share
-    normed_two_own = layer_norm(stream_own).astype(bf)
-    (normed_two,) = combined(
-        [(functools.partial(mp_peers, chips), functools.partial(mp_gather_body, chips), 1, 1, 2)],
-        [normed_two_own],
-        [sd((2, chips, 2) + normed_two_own.shape, bf)],
-        mp_gather_scratch(chips),
-        3,
-    )
     normed_two = normed_two.reshape(mp_count * rows, -1)
     upper = jnp.dot(normed_two, up_w, preferred_element_type=jnp.float32)
     activated = jax.nn.gelu(upper, approximate=True).astype(bf)
-    return (stream_own.astype(bf), activated, cache)
+    return (hidden_out, activated, cache)
 
 
 def solution(mesh):

time: 165 us -> 150 us (0.909)
  Pallas kernels: 141 us -> 129 us
  other arithmetic: 12.4 us -> 8.4 us
    pallas_call x3 -> x2, Pallas kernels: 141 us -> 129 us  [combined(): pl.pallas_call(functools.partial(combined_kernel, parts), out_shape=out_s...]
    convert_element_type x1 -> x0, other arithmetic: 1.66 us -> none  [local(): normed_two_own = layer_norm(stream_own).astype(bf)]
where the time goes in v10:
time: 150 us
  Pallas kernels  129 us (86%)
  matrix products  9.27 us (6%)
  other arithmetic  8.4 us (6%)
  local copies, waits for them, and re-layouts  2.45 us (2%)
    pallas_call x2, Pallas kernels, combined(): pl.pallas_call(functools.partial(combined_kernel, parts), out_shape=out_s...  129 us
    dot_general x1, matrix products, local(): upper = jnp.dot(normed_two, up_w, preferred_element_type=jnp.float32)  3.97 us

profile of v10, /device:TPU:1, one launch (start us, length us, event | category | flops | bytes accessed | tf_op | source)
XLA Modules:
  0.0 149.6 jit_solution(15258600691789371240)
XLA Ops:
  0.6 0.0 copy-start
  0.7 0.7 fusion.24
  1.4 1.0 convert_reduce_fusion
  2.4 1.1 fusion.19
  3.5 0.7 reduce.4
  4.2 1.5 %convert_element_type.43 = bf16[4,6144]{1,0:T(4,128)(2,1)} convert(f32[4,6144]{1,0:T(4,128)} %param.9) | non-fusion elementwise | flops 24576 | bytes 147456 | tf_op jit(solution)/shard_map/convert_element_type | solution.py:416
  5.8 1.6 %convert_element_type.44 = bf16[4,8192]{1,0:T(4,128)(2,1)} convert(f32[4,8192]{1,0:T(4,128)} %param.10) | non-fusion elementwise | flops 32768 | bytes 196608 | tf_op jit(solution)/shard_map/convert_element_type | solution.py:417
  7.3 1.6 %fusion.20.refs_2_ = bf16[24,2048]{1,0:T(8,128)(2,1)} fusion(bf16[24,2048]{1,0:T(8,128)(2,1)} %refs_1_.1, f32[24]{0:T(128)S(1)} %add_rsqrt_fusion, f32[24]{0:T(128)S(1)} %broadcast_multiply_fusion), kind=kLoop, calls=%fused_computation.30 | loop fusion | flops 196608 | bytes 196800 | tf_op jit(solution)/shard_map/convert_element_type | solution.py:418
  8.9 59.8 %shard_map.85 = (bf16[8,4,64,384]{3,2,1,0:T(8,128)(2,1)}, bf16[16,4,512]{2,1,0:T(4,128)(2,1)}, bf16[2,4,2,24,2048]{4,3,2,1,0:T(8,128)(2,1)}) custom-call(bf16[16,4,384]{2,1,0:T(4,128)(2,1)} %bitcast.58, bf16[16,4,512]{2,1,0:T(4,128)(2,1)} %bitcast.57, bf16[24,2048]{1,0:T(8,128)(2,1)} %fusion.20.refs_2_), custom_call_target="tpu_custom_call" | custom-call | tf_op jit(solution)/shard_map/pallas_call | solution.py:367
  68.8 0.0 copy-start.3
  68.8 2.9 %convolution_convert_fusion.1 = bf16[384,384]{0,1:T(8,128)(2,1)S(1)} fusion(bf16[384,2048]{1,0:T(8,128)(2,1)} %bitcast.64, bf16[2048,384]{1,0:T(8,128)(2,1)} %bitcast.63), kind=kOutput, calls=%fused_computation.5 | convolution fusion | flops 604127232 | bytes 3440640 | tf_op jit(solution)/shard_map/dot_general | solution.py:380
  71.7 0.0 copy-done.3
  71.7 0.6 reshape.135.refs_2_
  72.4 0.1 copy.15
  72.5 0.1 copy.14
  72.8 0.8 scatter_fusion
  73.6 0.0 copy-start.1
  73.6 0.4 fusion.29
  74.0 0.1 fusion.12
  74.1 0.0 copy-done
  74.1 2.0 %convolution_convert_fusion = bf16[384,2048]{1,0:T(8,128)(2,1)} fusion(bf16[128,2048]{1,0:T(8,128)(2,1)S(1)} %copy-done, f32[384,384]{0,1:T(8,128)S(1)} %get-tuple-element.24, f32[384]{0:T(512)S(1)} %fusion.12, f32[384]{0:T(512)S(1)} %get-tuple-element.23, bf16[384,1,3,128]{0,3,2,1:T(8,128)(2,1)S(1)} %bitcast.61), kind=kOutput, calls=%fused_computation.1 | convolution fusion | flops 240353280 | bytes 2789376 | tf_op jit(solution)/shard_map/dot_general | solution.py:446
  76.1 0.0 copy-done.1
  76.1 68.9 %shard_map.86 = (bf16[24,2048]{1,0:T(8,128)(2,1)}, bf16[2,4,2,24,2048]{4,3,2,1,0:T(8,128)(2,1)}, bf16[8,4,64,512]{3,2,1,0:T(8,128)(2,1)}) custom-call(bf16[2,4,2,24,2048]{4,3,2,1,0:T(8,128)(2,1)} %bitcast.54, bf16[24,2048]{1,0:T(8,128)(2,1)} %refs_1_.1, bf16[64,512]{1,0:T(8,128)(2,1)} %reshape.135.refs_2_), custom_call_target="tpu_custom_call" | custom-call | tf_op jit(solution)/shard_map/pallas_call | solution.py:367
  145.0 0.0 copy-start.2
  145.0 4.0 %fusion.10 = bf16[384,512]{1,0:T(8,128)(2,1)} fusion(bf16[384,2048]{1,0:T(8,128)(2,1)} %bitcast.65, bf16[2048,512]{1,0:T(8,128)(2,1)} %bitcast.62), kind=kOutput, calls=%fused_computation.16 | convolution fusion | flops 807075840 | bytes 4063232 | tf_op jit(solution)/shard_map/dot_general | solution.py:467
  149.0 0.0 copy-done.2
  149.0 0.6 copy.18
  (6 shorter events, 0.1 us)
Async XLA Ops:
  0.6 73.5 %copy-start = (bf16[128,2048]{1,0:T(8,128)(2,1)S(1)}, bf16[128,2048]{1,0:T(8,128)(2,1)}, u32[]{:S(2)}) copy-start(bf16[128,2048]{1,0:T(8,128)(2,1)} %param.11) | copy-start | bytes 1572868
  68.8 3.0 %copy-start.3 = (bf16[16,4,512]{2,1,0:T(4,128)(2,1)S(1)}, bf16[16,4,512]{2,1,0:T(4,128)(2,1)}, u32[]{:S(2)}) copy-start(bf16[16,4,512]{2,1,0:T(4,128)(2,1)} %get-tuple-element.11) | copy-start | bytes 196612
  73.6 2.5 %copy-start.1 = (bf16[3,2,128,128]{3,2,1,0:T(8,128)(2,1)}, bf16[3,2,128,128]{3,2,1,0:T(8,128)(2,1)S(1)}, u32[]{:S(2)}) copy-start(bf16[3,2,128,128]{3,2,1,0:T(8,128)(2,1)S(1)} %scatter_fusion) | copy-start | bytes 589828
  145.0 4.0 %copy-start.2 = (bf16[24,2048]{1,0:T(8,128)(2,1)S(1)}, bf16[24,2048]{1,0:T(8,128)(2,1)}, u32[]{:S(2)}) copy-start(bf16[24,2048]{1,0:T(8,128)(2,1)} %get-tuple-element.28) | copy-start | bytes 294916

commit v11 on v10

--- a/solution.py
+++ b/solution.py
@@ -225,6 +225,13 @@
     stream = h_ref[...].astype(jnp.float32) + share[...]
     hidden_ref[...] = stream.astype(hidden_ref.dtype)
     own[...] = layer_norm(stream).astype(own.dtype)
+    yield from mp_gather_body(chips, [own], [normed_ref], gather_scratch)
+
+
+def normed_gather_body(chips, ins, outs, scratch):
+    (h_ref,), (normed_ref,) = ins, outs
+    own, gather_scratch = scratch[0], scratch[1:]
+    own[...] = layer_norm(h_ref[...].astype(jnp.float32)).astype(own.dtype)
     yield from mp_gather_body(chips, [own], [normed_ref], gather_scratch)
 
 
@@ -415,7 +422,6 @@
     bf = jnp.bfloat16
     qkv_t = qkv_master.astype(bf).reshape(rows_w, mp_count, -1).transpose(1, 0, 2)
     up_t = up_master.astype(bf).reshape(rows_w, mp_count, -1).transpose(1, 0, 2)
-    normed_own = layer_norm(hidden_in.astype(jnp.float32)).astype(bf)
     sd = jax.ShapeDtypeStruct
     qkv_rows = sd((mp_count * rows_w, qkv_t.shape[-1]), bf)
     qkv_w, up_blk, normed = combined(
@@ -425,17 +431,18 @@
                 functools.partial(weights_body, mp_count, lines, RING),
                 2, 2, 7,
             ),
-            (functools.partial(mp_peers, chips), functools.partial(mp_gather_body, chips), 1, 1, 2),
+            (functools.partial(mp_peers, chips), functools.partial(normed_gather_body, chips), 1, 1, 3),
         ],
-        [qkv_t, up_t, normed_own],
+        [qkv_t, up_t, hidden_in],
         [
             sd((lines, RING) + qkv_rows.shape, bf),
             sd(up_t.shape, bf),
-            sd((2, chips, 2) + normed_own.shape, bf),
+            sd((2, chips, 2) + hidden_in.shape, bf),
         ],
         exchange_scratch(mp_count, 2)
         + [pltpu.VMEM(qkv_t.shape, bf), pltpu.VMEM(qkv_rows.shape, bf)]
         + dp_scratch(lines, RING)
+        + [pltpu.VMEM((rows, hidden_in.shape[-1]), bf)]
         + mp_gather_scratch(chips),
         1,
     )

time: 150 us -> 146 us (0.973)
  other arithmetic: 8.4 us -> 4.64 us
    reduce_sum x2 -> x0, other arithmetic: 2.12 us -> none  [the longest x1 1.1 us: layer_norm(): variance = jnp.mean(centered * centered, -1, keepdims=True)]
    convert_element_type x1 -> x0, other arithmetic: 1.62 us -> none  [local(): normed_own = layer_norm(hidden_in.astype(jnp.float32)).astype(bf)]
where the time goes in v11:
time: 146 us
  Pallas kernels  129 us (88%)
  matrix products  9.27 us (6%)
  other arithmetic  4.64 us (3%)
  local copies, waits for them, and re-layouts  2.45 us (2%)
    pallas_call x2, Pallas kernels, combined(): pl.pallas_call(functools.partial(combined_kernel, parts), out_shape=out_s...  129 us
    dot_general x1, matrix products, local(): upper = jnp.dot(normed_two, up_w, preferred_element_type=jnp.float32)  3.97 us
    dot_general x1, matrix products, attend(): jnp.dot(normed, qkv_w, preferred_element_type=jnp.float32)  2.94 us

profile of v11, /device:TPU:1, one launch (start us, length us, event | category | flops | bytes accessed | tf_op | source)
XLA Modules:
  0.0 145.9 jit_solution(8562360190602143716)
XLA Ops:
  0.6 0.0 copy-start
  0.7 0.7 fusion.20
  1.4 0.7 reduce.4
  2.1 1.5 %convert_element_type.37 = bf16[4,6144]{1,0:T(4,128)(2,1)} convert(f32[4,6144]{1,0:T(4,128)} %param.9) | non-fusion elementwise | flops 24576 | bytes 147456 | tf_op jit(solution)/shard_map/convert_element_type | solution.py:423
  3.6 1.6 %convert_element_type.38 = bf16[4,8192]{1,0:T(4,128)(2,1)} convert(f32[4,8192]{1,0:T(4,128)} %param.10) | non-fusion elementwise | flops 32768 | bytes 196608 | tf_op jit(solution)/shard_map/convert_element_type | solution.py:424
  5.2 59.8 %shard_map.85 = (bf16[8,4,64,384]{3,2,1,0:T(8,128)(2,1)}, bf16[16,4,512]{2,1,0:T(4,128)(2,1)}, bf16[2,4,2,24,2048]{4,3,2,1,0:T(8,128)(2,1)}) custom-call(bf16[16,4,384]{2,1,0:T(4,128)(2,1)} %bitcast.58, bf16[16,4,512]{2,1,0:T(4,128)(2,1)} %bitcast.57, bf16[24,2048]{1,0:T(8,128)(2,1)} %refs_1_.1), custom_call_target="tpu_custom_call" | custom-call | tf_op jit(solution)/shard_map/pallas_call | solution.py:374
  65.0 0.0 copy-start.3
  65.0 2.9 %convolution_convert_fusion.1 = bf16[384,384]{0,1:T(8,128)(2,1)S(1)} fusion(bf16[384,2048]{1,0:T(8,128)(2,1)} %bitcast.64, bf16[2048,384]{1,0:T(8,128)(2,1)} %bitcast.63), kind=kOutput, calls=%fused_computation.5 | convolution fusion | flops 604127232 | bytes 3440640 | tf_op jit(solution)/shard_map/dot_general | solution.py:387
  68.0 0.0 copy-done.3
  68.0 0.6 reshape.123.refs_2_
  68.7 0.1 copy.15
  68.8 0.1 copy.14
  69.0 0.8 scatter_fusion
  69.8 0.0 copy-start.1
  69.8 0.4 fusion.25
  70.2 0.1 fusion.12
  70.4 0.0 copy-done
  70.4 2.0 %convolution_convert_fusion = bf16[384,2048]{1,0:T(8,128)(2,1)} fusion(bf16[128,2048]{1,0:T(8,128)(2,1)S(1)} %copy-done, f32[384,384]{0,1:T(8,128)S(1)} %get-tuple-element.24, f32[384]{0:T(512)S(1)} %fusion.12, f32[384]{0:T(512)S(1)} %get-tuple-element.23, bf16[384,1,3,128]{0,3,2,1:T(8,128)(2,1)S(1)} %bitcast.61), kind=kOutput, calls=%fused_computation.1 | convolution fusion | flops 240353280 | bytes 2789376 | tf_op jit(solution)/shard_map/dot_general | solution.py:453
  72.3 0.0 copy-done.1
  72.3 68.9 %shard_map.86 = (bf16[24,2048]{1,0:T(8,128)(2,1)}, bf16[2,4,2,24,2048]{4,3,2,1,0:T(8,128)(2,1)}, bf16[8,4,64,512]{3,2,1,0:T(8,128)(2,1)}) custom-call(bf16[2,4,2,24,2048]{4,3,2,1,0:T(8,128)(2,1)} %bitcast.54, bf16[24,2048]{1,0:T(8,128)(2,1)} %refs_1_.1, bf16[64,512]{1,0:T(8,128)(2,1)} %reshape.123.refs_2_), custom_call_target="tpu_custom_call" | custom-call | tf_op jit(solution)/shard_map/pallas_call | solution.py:374
  141.2 0.0 copy-start.2
  141.3 4.0 %fusion.10 = bf16[384,512]{1,0:T(8,128)(2,1)} fusion(bf16[384,2048]{1,0:T(8,128)(2,1)} %bitcast.65, bf16[2048,512]{1,0:T(8,128)(2,1)} %bitcast.62), kind=kOutput, calls=%fused_computation.16 | convolution fusion | flops 807075840 | bytes 4063232 | tf_op jit(solution)/shard_map/dot_general | solution.py:474
  145.2 0.0 copy-done.2
  145.2 0.6 copy.18
  (4 shorter events, 0.1 us)
Async XLA Ops:
  0.6 69.7 %copy-start = (bf16[128,2048]{1,0:T(8,128)(2,1)S(1)}, bf16[128,2048]{1,0:T(8,128)(2,1)}, u32[]{:S(2)}) copy-start(bf16[128,2048]{1,0:T(8,128)(2,1)} %param.11) | copy-start | bytes 1572868
  65.0 3.0 %copy-start.3 = (bf16[16,4,512]{2,1,0:T(4,128)(2,1)S(1)}, bf16[16,4,512]{2,1,0:T(4,128)(2,1)}, u32[]{:S(2)}) copy-start(bf16[16,4,512]{2,1,0:T(4,128)(2,1)} %get-tuple-element.11) | copy-start | bytes 196612
  69.8 2.5 %copy-start.1 = (bf16[3,2,128,128]{3,2,1,0:T(8,128)(2,1)}, bf16[3,2,128,128]{3,2,1,0:T(8,128)(2,1)S(1)}, u32[]{:S(2)}) copy-start(bf16[3,2,128,128]{3,2,1,0:T(8,128)(2,1)S(1)} %scatter_fusion) | copy-start | bytes 589828
  141.2 4.0 %copy-start.2 = (bf16[24,2048]{1,0:T(8,128)(2,1)S(1)}, bf16[24,2048]{1,0:T(8,128)(2,1)}, u32[]{:S(2)}) copy-start(bf16[24,2048]{1,0:T(8,128)(2,1)} %get-tuple-element.28) | copy-start | bytes 294916

commit v12 on v11

--- a/solution.py
+++ b/solution.py
@@ -205,8 +205,12 @@
 
 
 def weights_body(n, lines, ring, ins, outs, scratch):
-    (qkv_t, up_t), (qkv_full, up_blk) = ins, outs
-    ex_send, ex_recv, ex_local, qkv_blk, qkv_rows, dp_send, dp_recv = scratch
+    (qkv_m, up_m), (qkv_full, up_blk) = ins, outs
+    ex_send, ex_recv, ex_local, qkv_blk, qkv_rows, dp_send, dp_recv, qkv_t, up_t = scratch
+    for master, cast in ((qkv_m, qkv_t), (up_m, up_t)):
+        width = cast.shape[-1]
+        for m in range(n):
+            cast[m] = master[:, m * width:(m + 1) * width].astype(cast.dtype)
     yield from exchange_body(n, "mp", [qkv_t, up_t], [qkv_blk, up_blk], (ex_send, ex_recv, ex_local))
     per = qkv_blk.shape[1]
     for m in range(n):
@@ -420,20 +424,20 @@
     rows = hidden_in.shape[0]
     rows_w = qkv_master.shape[0]
     bf = jnp.bfloat16
-    qkv_t = qkv_master.astype(bf).reshape(rows_w, mp_count, -1).transpose(1, 0, 2)
-    up_t = up_master.astype(bf).reshape(rows_w, mp_count, -1).transpose(1, 0, 2)
     sd = jax.ShapeDtypeStruct
+    qkv_t = sd((mp_count, rows_w, qkv_master.shape[-1] // mp_count), bf)
+    up_t = sd((mp_count, rows_w, up_master.shape[-1] // mp_count), bf)
     qkv_rows = sd((mp_count * rows_w, qkv_t.shape[-1]), bf)
     qkv_w, up_blk, normed = combined(
         [
             (
                 functools.partial(weights_peers, mp_count, lines, RING),
                 functools.partial(weights_body, mp_count, lines, RING),
-                2, 2, 7,
+                2, 2, 9,
             ),
             (functools.partial(mp_peers, chips), functools.partial(normed_gather_body, chips), 1, 1, 3),
         ],
-        [qkv_t, up_t, hidden_in],
+        [qkv_master, up_master, hidden_in],
         [
             sd((lines, RING) + qkv_rows.shape, bf),
             sd(up_t.shape, bf),
@@ -442,6 +446,7 @@
         exchange_scratch(mp_count, 2)
         + [pltpu.VMEM(qkv_t.shape, bf), pltpu.VMEM(qkv_rows.shape, bf)]
         + dp_scratch(lines, RING)
+        + [pltpu.VMEM(qkv_t.shape, bf), pltpu.VMEM(up_t.shape, bf)]
         + [pltpu.VMEM((rows, hidden_in.shape[-1]), bf)]
         + mp_gather_scratch(chips),
         1,

time: 146 us -> 143 us (0.979)
  other arithmetic: 4.64 us -> 1.55 us
    convert_element_type x2 -> x0, other arithmetic: 3.09 us -> none  [the longest x1 1.56 us: local(): up_t = up_master.astype(bf).reshape(rows_w, mp_count, -1).transpose(1, 0, 2)]
where the time goes in v12:
time: 143 us
  Pallas kernels  129 us (90%)
  matrix products  9.27 us (6%)
  local copies, waits for them, and re-layouts  2.45 us (2%)
  other arithmetic  1.55 us (1%)
    pallas_call x2, Pallas kernels, combined(): pl.pallas_call(functools.partial(combined_kernel, parts), out_shape=out_s...  129 us
    dot_general x1, matrix products, local(): upper = jnp.dot(normed_two, up_w, preferred_element_type=jnp.float32)  3.97 us
    dot_general x1, matrix products, attend(): jnp.dot(normed, qkv_w, preferred_element_type=jnp.float32)  2.94 us

profile of v12, /device:TPU:1, one launch (start us, length us, event | category | flops | bytes accessed | tf_op | source)
XLA Modules:
  0.0 142.9 jit_solution(5603802937424869547)
XLA Ops:
  0.6 0.0 copy-start
  0.7 0.7 fusion.20
  1.4 0.7 reduce.4
  2.1 59.9 %shard_map.85 = (bf16[8,4,64,384]{3,2,1,0:T(8,128)(2,1)}, bf16[16,4,512]{2,1,0:T(4,128)(2,1)}, bf16[2,4,2,24,2048]{4,3,2,1,0:T(8,128)(2,1)}) custom-call(f32[4,6144]{1,0:T(4,128)} %refs_0_.1, f32[4,8192]{1,0:T(4,128)} %refs_1_.2, bf16[24,2048]{1,0:T(8,128)(2,1)} %refs_1_.3), custom_call_target="tpu_custom_call" | custom-call | tf_op jit(solution)/shard_map/pallas_call | solution.py:378
  62.0 0.0 copy-start.3
  62.0 2.9 %convolution_convert_fusion.1 = bf16[384,384]{0,1:T(8,128)(2,1)S(1)} fusion(bf16[384,2048]{1,0:T(8,128)(2,1)} %bitcast.57, bf16[2048,384]{1,0:T(8,128)(2,1)} %bitcast.56), kind=kOutput, calls=%fused_computation.5 | convolution fusion | flops 604127232 | bytes 3440640 | tf_op jit(solution)/shard_map/dot_general | solution.py:391
  65.0 0.0 copy-done.3
  65.0 0.6 reshape.115.refs_2_
  65.7 0.1 copy.15
  65.8 0.1 copy.14
  66.0 0.8 scatter_fusion
  66.9 0.0 copy-start.1
  66.9 0.4 fusion.25
  67.3 0.1 fusion.12
  67.4 0.0 copy-done
  67.4 2.0 %convolution_convert_fusion = bf16[384,2048]{1,0:T(8,128)(2,1)} fusion(bf16[128,2048]{1,0:T(8,128)(2,1)S(1)} %copy-done, f32[384,384]{0,1:T(8,128)S(1)} %get-tuple-element.24, f32[384]{0:T(512)S(1)} %fusion.12, f32[384]{0:T(512)S(1)} %get-tuple-element.23, bf16[384,1,3,128]{0,3,2,1:T(8,128)(2,1)S(1)} %bitcast.53), kind=kOutput, calls=%fused_computation.1 | convolution fusion | flops 240353280 | bytes 2789376 | tf_op jit(solution)/shard_map/dot_general | solution.py:458
  69.4 0.0 copy-done.1
  69.4 68.9 %shard_map.86 = (bf16[24,2048]{1,0:T(8,128)(2,1)}, bf16[2,4,2,24,2048]{4,3,2,1,0:T(8,128)(2,1)}, bf16[8,4,64,512]{3,2,1,0:T(8,128)(2,1)}) custom-call(bf16[2,4,2,24,2048]{4,3,2,1,0:T(8,128)(2,1)} %bitcast.48, bf16[24,2048]{1,0:T(8,128)(2,1)} %refs_1_.3, bf16[64,512]{1,0:T(8,128)(2,1)} %reshape.115.refs_2_), custom_call_target="tpu_custom_call" | custom-call | tf_op jit(solution)/shard_map/pallas_call | solution.py:378
  138.3 0.0 copy-start.2
  138.3 4.0 %fusion.10 = bf16[384,512]{1,0:T(8,128)(2,1)} fusion(bf16[384,2048]{1,0:T(8,128)(2,1)} %bitcast.55, bf16[2048,512]{1,0:T(8,128)(2,1)} %bitcast.54), kind=kOutput, calls=%fused_computation.16 | convolution fusion | flops 807075840 | bytes 4063232 | tf_op jit(solution)/shard_map/dot_general | solution.py:479
  142.3 0.0 copy-done.2
  142.3 0.6 copy.18
  (4 shorter events, 0.1 us)
Async XLA Ops:
  0.6 66.8 %copy-start = (bf16[128,2048]{1,0:T(8,128)(2,1)S(1)}, bf16[128,2048]{1,0:T(8,128)(2,1)}, u32[]{:S(2)}) copy-start(bf16[128,2048]{1,0:T(8,128)(2,1)} %param.11) | copy-start | bytes 1572868
  62.0 3.0 %copy-start.3 = (bf16[16,4,512]{2,1,0:T(4,128)(2,1)S(1)}, bf16[16,4,512]{2,1,0:T(4,128)(2,1)}, u32[]{:S(2)}) copy-start(bf16[16,4,512]{2,1,0:T(4,128)(2,1)} %get-tuple-element.11) | copy-start | bytes 196612
  66.9 2.5 %copy-start.1 = (bf16[3,2,128,128]{3,2,1,0:T(8,128)(2,1)}, bf16[3,2,128,128]{3,2,1,0:T(8,128)(2,1)S(1)}, u32[]{:S(2)}) copy-start(bf16[3,2,128,128]{3,2,1,0:T(8,128)(2,1)S(1)} %scatter_fusion) | copy-start | bytes 589828
  138.3 4.0 %copy-start.2 = (bf16[24,2048]{1,0:T(8,128)(2,1)S(1)}, bf16[24,2048]{1,0:T(8,128)(2,1)}, u32[]{:S(2)}) copy-start(bf16[24,2048]{1,0:T(8,128)(2,1)} %get-tuple-element.28) | copy-start | bytes 294916

commit v13 on v12

--- a/solution.py
+++ b/solution.py
@@ -205,17 +205,29 @@
 
 
 def weights_body(n, lines, ring, ins, outs, scratch):
-    (qkv_m, up_m), (qkv_full, up_blk) = ins, outs
-    ex_send, ex_recv, ex_local, qkv_blk, qkv_rows, dp_send, dp_recv, qkv_t, up_t = scratch
+    (qkv_m, up_m), (qkv_full, up_full) = ins, outs
+    ex_send, ex_recv, ex_local, qkv_t, up_t, qkv_blk, up_blk, qkv_rows, up_rows = scratch[:9]
+    dp_qkv, dp_up = scratch[9:11], scratch[11:13]
     for master, cast in ((qkv_m, qkv_t), (up_m, up_t)):
         width = cast.shape[-1]
         for m in range(n):
             cast[m] = master[:, m * width:(m + 1) * width].astype(cast.dtype)
     yield from exchange_body(n, "mp", [qkv_t, up_t], [qkv_blk, up_blk], (ex_send, ex_recv, ex_local))
-    per = qkv_blk.shape[1]
-    for m in range(n):
-        qkv_rows[m * per:(m + 1) * per, :] = qkv_blk[m]
-    yield from dp_gather_body(lines, ring, [qkv_rows], [qkv_full], (dp_send, dp_recv))
+    for blk, rows_buf in ((qkv_blk, qkv_rows), (up_blk, up_rows)):
+        per = blk.shape[1]
+        for m in range(n):
+            rows_buf[m * per:(m + 1) * per, :] = blk[m]
+    gens = [
+        dp_gather_body(lines, ring, [qkv_rows], [qkv_full], dp_qkv),
+        dp_gather_body(lines, ring, [up_rows], [up_full], dp_up),
+    ]
+    while gens:
+        for gen in list(gens):
+            try:
+                next(gen)
+            except StopIteration:
+                gens.remove(gen)
+        yield
 
 
 def tail_peers(chips):
@@ -428,53 +440,45 @@
     qkv_t = sd((mp_count, rows_w, qkv_master.shape[-1] // mp_count), bf)
     up_t = sd((mp_count, rows_w, up_master.shape[-1] // mp_count), bf)
     qkv_rows = sd((mp_count * rows_w, qkv_t.shape[-1]), bf)
-    qkv_w, up_blk, normed = combined(
+    up_rows = sd((mp_count * rows_w, up_t.shape[-1]), bf)
+    qkv_w, up_w, normed = combined(
         [
             (
                 functools.partial(weights_peers, mp_count, lines, RING),
                 functools.partial(weights_body, mp_count, lines, RING),
-                2, 2, 9,
+                2, 2, 13,
             ),
             (functools.partial(mp_peers, chips), functools.partial(normed_gather_body, chips), 1, 1, 3),
         ],
         [qkv_master, up_master, hidden_in],
         [
             sd((lines, RING) + qkv_rows.shape, bf),
-            sd(up_t.shape, bf),
+            sd((lines, RING) + up_rows.shape, bf),
             sd((2, chips, 2) + hidden_in.shape, bf),
         ],
         exchange_scratch(mp_count, 2)
-        + [pltpu.VMEM(qkv_t.shape, bf), pltpu.VMEM(qkv_rows.shape, bf)]
+        + [pltpu.VMEM(x.shape, bf) for x in (qkv_t, up_t, qkv_t, up_t, qkv_rows, up_rows)]
         + dp_scratch(lines, RING)
-        + [pltpu.VMEM(qkv_t.shape, bf), pltpu.VMEM(up_t.shape, bf)]
+        + dp_scratch(lines, RING)
         + [pltpu.VMEM((rows, hidden_in.shape[-1]), bf)]
         + mp_gather_scratch(chips),
         1,
     )
     normed = normed.reshape(mp_count * rows, -1)
     qkv_w = qkv_w.reshape(-1, qkv_t.shape[-1])
-    up_piece = up_blk.reshape(mp_count * rows_w, -1)
+    up_w = up_w.reshape(-1, up_t.shape[-1])
     context, cache = attend(normed, qkv_w, segment_ids[0], page_table[0], mp_index)
     partial = jnp.dot(context, dense_weight, preferred_element_type=jnp.float32).astype(bf)
     cols = partial.shape[-1]
-    hidden_out, normed_two, up_w = combined(
-        [
-            (functools.partial(tail_peers, chips), functools.partial(tail_body, chips), 2, 2, 12),
-            (functools.partial(dp_peers, lines, RING), functools.partial(dp_gather_body, lines, RING), 1, 1, 2),
-        ],
-        [partial.reshape(2, chips, 2, rows, -1), hidden_in, up_piece],
-        [
-            sd((rows, cols), bf),
-            sd((2, chips, 2, rows, cols), bf),
-            sd((lines, RING) + up_piece.shape, bf),
-        ],
+    hidden_out, normed_two = combined(
+        [(functools.partial(tail_peers, chips), functools.partial(tail_body, chips), 2, 2, 12)],
+        [partial.reshape(2, chips, 2, rows, -1), hidden_in],
+        [sd((rows, cols), bf), sd((2, chips, 2, rows, cols), bf)],
         mp_sum_scratch(chips, rows, cols, bf)
         + [pltpu.VMEM((rows, cols), jnp.float32), pltpu.VMEM((rows, cols), bf)]
-        + mp_gather_scratch(chips)
-        + dp_scratch(lines, RING),
+        + mp_gather_scratch(chips),
         2,
     )
-    up_w = up_w.reshape(-1, up_piece.shape[-1])
     normed_two = normed_two.reshape(mp_count * rows, -1)
     upper = jnp.dot(normed_two, up_w, preferred_element_type=jnp.float32)
     activated = jax.nn.gelu(upper, approximate=True).astype(bf)

time: 143 us -> 149 us (1.042)
  Pallas kernels: 129 us -> 137 us
    pallas_call x2, Pallas kernels: 129 us -> 137 us  [combined(): pl.pallas_call(functools.partial(combined_kernel, parts), out_shape=out_s...]
where the time goes in v13:
time: 149 us; the launch traced here: 148 us
  Pallas kernels  137 us (92%)
  matrix products  8.59 us (6%)
  local copies, waits for them, and re-layouts  2.18 us (1%)
    pallas_call x2, Pallas kernels, combined(): pl.pallas_call(functools.partial(combined_kernel, parts), out_shape=out_s...  137 us
    dot_general x1, matrix products, local(): upper = jnp.dot(normed_two, up_w, preferred_element_type=jnp.float32)  3.28 us

profile of v13, /device:TPU:1, one launch (start us, length us, event | category | flops | bytes accessed | tf_op | source)
XLA Modules:
  0.0 148.4 jit_solution(5740379544891383164)
XLA Ops:
  0.6 0.0 copy-start
  0.6 77.9 %shard_map.85 = (bf16[8,4,64,384]{3,2,1,0:T(8,128)(2,1)}, bf16[8,4,64,512]{3,2,1,0:T(8,128)(2,1)}, bf16[2,4,2,24,2048]{4,3,2,1,0:T(8,128)(2,1)}) custom-call(f32[4,6144]{1,0:T(4,128)} %refs_0_.1, f32[4,8192]{1,0:T(4,128)} %refs_1_.2, bf16[24,2048]{1,0:T(8,128)(2,1)} %refs_1_.3), custom_call_target="tpu_custom_call" | custom-call | tf_op jit(solution)/shard_map/pallas_call | solution.py:390
  78.6 0.0 copy-start.3
  78.6 2.9 %convolution_convert_fusion.1 = bf16[384,384]{0,1:T(8,128)(2,1)S(1)} fusion(bf16[384,2048]{1,0:T(8,128)(2,1)} %bitcast.56, bf16[2048,384]{1,0:T(8,128)(2,1)} %bitcast.55), kind=kOutput, calls=%fused_computation.5 | convolution fusion | flops 604127232 | bytes 3440640 | tf_op jit(solution)/shard_map/dot_general | solution.py:403
  81.6 0.0 copy-done.3
  81.6 0.4 fusion.25
  82.0 0.1 fusion.12
  82.1 0.0 copy-done
  82.1 0.0 copy-start.4
  82.1 2.0 %convolution_convert_fusion = bf16[384,2048]{1,0:T(8,128)(2,1)} fusion(bf16[128,2048]{1,0:T(8,128)(2,1)S(1)} %copy-done, f32[384,384]{0,1:T(8,128)S(1)} %get-tuple-element.22, f32[384]{0:T(512)S(1)} %fusion.12, f32[384]{0:T(512)S(1)} %get-tuple-element.21, bf16[384,1,3,128]{0,3,2,1:T(8,128)(2,1)S(1)} %bitcast.51), kind=kOutput, calls=%fused_computation.1 | convolution fusion | flops 240353280 | bytes 2789376 | tf_op jit(solution)/shard_map/dot_general | solution.py:471
  84.1 58.7 %shard_map.86 = (bf16[24,2048]{1,0:T(8,128)(2,1)}, bf16[2,4,2,24,2048]{4,3,2,1,0:T(8,128)(2,1)}) custom-call(bf16[2,4,2,24,2048]{4,3,2,1,0:T(8,128)(2,1)} %bitcast.47, bf16[24,2048]{1,0:T(8,128)(2,1)} %refs_1_.3), custom_call_target="tpu_custom_call" | custom-call | tf_op jit(solution)/shard_map/pallas_call | solution.py:390
  142.9 0.0 copy-done.4
  142.9 3.3 %fusion.10 = bf16[384,512]{1,0:T(8,128)(2,1)} fusion(bf16[384,2048]{1,0:T(8,128)(2,1)} %bitcast.54, bf16[2048,512]{1,0:T(8,128)(2,1)S(1)} %bitcast.53), kind=kOutput, calls=%fused_computation.16 | convolution fusion | flops 807075840 | bytes 4063232 | tf_op jit(solution)/shard_map/dot_general | solution.py:483
  146.2 0.0 copy-start.5
  146.2 0.0 copy-start.2
  146.2 0.1 copy.14
  146.3 0.1 copy.15
  146.5 0.3 copy-done.5
  146.8 0.8 scatter_fusion
  147.7 0.0 copy-start.1
  147.7 0.0 copy-done.2
  147.7 0.7 copy.18
  148.4 0.0 copy-done.1
  (6 shorter events, 0.1 us)
Async XLA Ops:
  0.6 81.5 %copy-start = (bf16[128,2048]{1,0:T(8,128)(2,1)S(1)}, bf16[128,2048]{1,0:T(8,128)(2,1)}, u32[]{:S(2)}) copy-start(bf16[128,2048]{1,0:T(8,128)(2,1)} %param.11) | copy-start | bytes 1572868
  78.6 3.0 %copy-start.3 = (s32[1,384]{1,0:T(1,128)S(1)}, s32[1,384]{1,0:T(1,128)}, u32[]{:S(2)}) copy-start(s32[1,384]{1,0:T(1,128)} %param.7) | copy-start | bytes 4612
  82.1 60.7 %copy-start.4 = (bf16[8,4,64,512]{3,2,1,0:T(8,128)(2,1)S(1)}, bf16[8,4,64,512]{3,2,1,0:T(8,128)(2,1)}, u32[]{:S(2)}) copy-start(bf16[8,4,64,512]{3,2,1,0:T(8,128)(2,1)} %get-tuple-element.12) | copy-start | bytes 6291460
  146.2 0.7 copy-start.5
  146.2 1.5 %copy-start.2 = (bf16[24,2048]{1,0:T(8,128)(2,1)S(1)}, bf16[24,2048]{1,0:T(8,128)(2,1)}, u32[]{:S(2)}) copy-start(bf16[24,2048]{1,0:T(8,128)(2,1)} %get-tuple-element.26) | copy-start | bytes 294916
  147.7 0.7 copy-start.1

commit v14 on v12

--- a/solution.py
+++ b/solution.py
@@ -457,21 +457,21 @@
     context, cache = attend(normed, qkv_w, segment_ids[0], page_table[0], mp_index)
     partial = jnp.dot(context, dense_weight, preferred_element_type=jnp.float32).astype(bf)
     cols = partial.shape[-1]
-    hidden_out, normed_two, up_w = combined(
+    up_w, hidden_out, normed_two = combined(
         [
+            (functools.partial(dp_peers, lines, RING), functools.partial(dp_gather_body, lines, RING), 1, 1, 2),
             (functools.partial(tail_peers, chips), functools.partial(tail_body, chips), 2, 2, 12),
-            (functools.partial(dp_peers, lines, RING), functools.partial(dp_gather_body, lines, RING), 1, 1, 2),
         ],
-        [partial.reshape(2, chips, 2, rows, -1), hidden_in, up_piece],
+        [up_piece, partial.reshape(2, chips, 2, rows, -1), hidden_in],
         [
+            sd((lines, RING) + up_piece.shape, bf),
             sd((rows, cols), bf),
             sd((2, chips, 2, rows, cols), bf),
-            sd((lines, RING) + up_piece.shape, bf),
         ],
-        mp_sum_scratch(chips, rows, cols, bf)
+        dp_scratch(lines, RING)
+        + mp_sum_scratch(chips, rows, cols, bf)
         + [pltpu.VMEM((rows, cols), jnp.float32), pltpu.VMEM((rows, cols), bf)]
-        + mp_gather_scratch(chips)
-        + dp_scratch(lines, RING),
+        + mp_gather_scratch(chips),
         2,
     )
     up_w = up_w.reshape(-1, up_piece.shape[-1])

time: 143 us -> 142 us (level)
  Pallas kernels: 129 us -> 126 us
    pallas_call x2, Pallas kernels: 129 us -> 126 us  [combined(): pl.pallas_call(functools.partial(combined_kernel, parts), out_shape=out_s...]
where the time goes in v14:
time: 142 us; the launch traced here: 141 us
  Pallas kernels  126 us (89%)
  matrix products  9.24 us (7%)
  local copies, waits for them, and re-layouts  3.29 us (2%)
  other arithmetic  1.55 us (1%)
    pallas_call x2, Pallas kernels, combined(): pl.pallas_call(functools.partial(combined_kernel, parts), out_shape=out_s...  126 us
    dot_general x1, matrix products, local(): upper = jnp.dot(normed_two, up_w, preferred_element_type=jnp.float32)  3.97 us
    dot_general x1, matrix products, attend(): jnp.dot(normed, qkv_w, preferred_element_type=jnp.float32)  2.9 us

profile of v14, /device:TPU:1, one launch (start us, length us, event | category | flops | bytes accessed | tf_op | source)
XLA Modules:
  0.0 140.8 jit_solution(4360621779830879430)
XLA Ops:
  0.6 0.0 copy-start
  0.7 0.7 fusion.20
  1.4 0.7 reduce.4
  2.1 59.9 %shard_map.85 = (bf16[8,4,64,384]{3,2,1,0:T(8,128)(2,1)}, bf16[16,4,512]{2,1,0:T(4,128)(2,1)}, bf16[2,4,2,24,2048]{4,3,2,1,0:T(8,128)(2,1)}) custom-call(f32[4,6144]{1,0:T(4,128)} %refs_0_.1, f32[4,8192]{1,0:T(4,128)} %refs_1_.1, bf16[24,2048]{1,0:T(8,128)(2,1)} %refs_2_.3), custom_call_target="tpu_custom_call" | custom-call | tf_op jit(solution)/shard_map/pallas_call | solution.py:378
  62.0 1.5 %reshape.107.refs_0_ = bf16[64,512]{1,0:T(8,128)(2,1)} reshape(bf16[16,4,512]{2,1,0:T(4,128)(2,1)} %get-tuple-element.9) | data formatting | bytes 131072 | tf_op jit(solution)/shard_map/reshape | solution.py:456
  63.5 2.9 %convolution_convert_fusion.1 = bf16[384,384]{0,1:T(8,128)(2,1)S(1)} fusion(bf16[384,2048]{1,0:T(8,128)(2,1)} %bitcast.57, bf16[2048,384]{1,0:T(8,128)(2,1)} %bitcast.56), kind=kOutput, calls=%fused_computation.5 | convolution fusion | flops 604127232 | bytes 3440640 | tf_op jit(solution)/shard_map/dot_general | solution.py:391
  66.5 0.1 copy.15
  66.6 0.1 copy.14
  66.8 0.8 scatter_fusion
  67.6 0.0 copy-start.1
  67.7 0.4 fusion.25
  68.1 0.1 fusion.12
  68.2 0.0 copy-done
  68.2 2.0 %convolution_convert_fusion = bf16[384,2048]{1,0:T(8,128)(2,1)} fusion(bf16[128,2048]{1,0:T(8,128)(2,1)S(1)} %copy-done, f32[384,384]{0,1:T(8,128)S(1)} %get-tuple-element.24, f32[384]{0:T(512)S(1)} %fusion.12, f32[384]{0:T(512)S(1)} %get-tuple-element.23, bf16[384,1,3,128]{0,3,2,1:T(8,128)(2,1)S(1)} %bitcast.53), kind=kOutput, calls=%fused_computation.1 | convolution fusion | flops 240353280 | bytes 2789376 | tf_op jit(solution)/shard_map/dot_general | solution.py:458
  70.2 0.0 copy-done.1
  70.2 66.0 %shard_map.86 = (bf16[8,4,64,512]{3,2,1,0:T(8,128)(2,1)}, bf16[24,2048]{1,0:T(8,128)(2,1)}, bf16[2,4,2,24,2048]{4,3,2,1,0:T(8,128)(2,1)}) custom-call(bf16[64,512]{1,0:T(8,128)(2,1)} %reshape.107.refs_0_, bf16[2,4,2,24,2048]{4,3,2,1,0:T(8,128)(2,1)} %bitcast.48, bf16[24,2048]{1,0:T(8,128)(2,1)} %refs_2_.3), custom_call_target="tpu_custom_call" | custom-call | tf_op jit(solution)/shard_map/pallas_call | solution.py:378
  136.2 0.0 copy-start.2
  136.2 4.0 %fusion.10 = bf16[384,512]{1,0:T(8,128)(2,1)} fusion(bf16[384,2048]{1,0:T(8,128)(2,1)} %bitcast.55, bf16[2048,512]{1,0:T(8,128)(2,1)} %bitcast.54), kind=kOutput, calls=%fused_computation.16 | convolution fusion | flops 807075840 | bytes 4063232 | tf_op jit(solution)/shard_map/dot_general | solution.py:479
  140.1 0.0 copy-done.2
  140.1 0.6 copy.18
  (4 shorter events, 0.1 us)
Async XLA Ops:
  0.6 67.6 %copy-start = (bf16[128,2048]{1,0:T(8,128)(2,1)S(1)}, bf16[128,2048]{1,0:T(8,128)(2,1)}, u32[]{:S(2)}) copy-start(bf16[128,2048]{1,0:T(8,128)(2,1)} %param.11) | copy-start | bytes 1572868
  67.6 2.5 %copy-start.1 = (bf16[3,2,128,128]{3,2,1,0:T(8,128)(2,1)}, bf16[3,2,128,128]{3,2,1,0:T(8,128)(2,1)S(1)}, u32[]{:S(2)}) copy-start(bf16[3,2,128,128]{3,2,1,0:T(8,128)(2,1)S(1)} %scatter_fusion) | copy-start | bytes 589828
  136.2 4.0 %copy-start.2 = (bf16[24,2048]{1,0:T(8,128)(2,1)S(1)}, bf16[24,2048]{1,0:T(8,128)(2,1)}, u32[]{:S(2)}) copy-start(bf16[24,2048]{1,0:T(8,128)(2,1)} %get-tuple-element.28) | copy-start | bytes 294916

commit v15 on v14

--- a/solution.py
+++ b/solution.py
@@ -205,8 +205,8 @@
 
 
 def weights_body(n, lines, ring, ins, outs, scratch):
-    (qkv_m, up_m), (qkv_full, up_blk) = ins, outs
-    ex_send, ex_recv, ex_local, qkv_blk, qkv_rows, dp_send, dp_recv, qkv_t, up_t = scratch
+    (qkv_m, up_m), (qkv_full, up_rows) = ins, outs
+    ex_send, ex_recv, ex_local, qkv_blk, qkv_rows, dp_send, dp_recv, qkv_t, up_t, up_blk = scratch
     for master, cast in ((qkv_m, qkv_t), (up_m, up_t)):
         width = cast.shape[-1]
         for m in range(n):
@@ -215,6 +215,7 @@
     per = qkv_blk.shape[1]
     for m in range(n):
         qkv_rows[m * per:(m + 1) * per, :] = qkv_blk[m]
+        up_rows[m * per:(m + 1) * per, :] = up_blk[m]
     yield from dp_gather_body(lines, ring, [qkv_rows], [qkv_full], (dp_send, dp_recv))
 
 
@@ -433,27 +434,27 @@
             (
                 functools.partial(weights_peers, mp_count, lines, RING),
                 functools.partial(weights_body, mp_count, lines, RING),
-                2, 2, 9,
+                2, 2, 10,
             ),
             (functools.partial(mp_peers, chips), functools.partial(normed_gather_body, chips), 1, 1, 3),
         ],
         [qkv_master, up_master, hidden_in],
         [
             sd((lines, RING) + qkv_rows.shape, bf),
-            sd(up_t.shape, bf),
+            sd((mp_count * rows_w, up_t.shape[-1]), bf),
             sd((2, chips, 2) + hidden_in.shape, bf),
         ],
         exchange_scratch(mp_count, 2)
         + [pltpu.VMEM(qkv_t.shape, bf), pltpu.VMEM(qkv_rows.shape, bf)]
         + dp_scratch(lines, RING)
-        + [pltpu.VMEM(qkv_t.shape, bf), pltpu.VMEM(up_t.shape, bf)]
+        + [pltpu.VMEM(qkv_t.shape, bf), pltpu.VMEM(up_t.shape, bf), pltpu.VMEM(up_t.shape, bf)]
         + [pltpu.VMEM((rows, hidden_in.shape[-1]), bf)]
         + mp_gather_scratch(chips),
         1,
     )
     normed = normed.reshape(mp_count * rows, -1)
     qkv_w = qkv_w.reshape(-1, qkv_t.shape[-1])
-    up_piece = up_blk.reshape(mp_count * rows_w, -1)
+    up_piece = up_blk
     context, cache = attend(normed, qkv_w, segment_ids[0], page_table[0], mp_index)
     partial = jnp.dot(context, dense_weight, preferred_element_type=jnp.float32).astype(bf)
     cols = partial.shape[-1]

time: 142 us -> 141 us (level)
  local copies, waits for them, and re-layouts: 3.29 us -> 1.8 us
    reshape x1 -> x0, local copies, waits for them, and re-layouts: 1.49 us -> none  [local(): up_piece = up_blk.reshape(mp_count * rows_w, -1)]
where the time goes in v15:
time: 141 us; the launch traced here: 139 us
  Pallas kernels  126 us (89%)
  matrix products  9.23 us (7%)
  local copies, waits for them, and re-layouts  1.8 us (1%)
  other arithmetic  1.55 us (1%)
    pallas_call x2, Pallas kernels, combined(): pl.pallas_call(functools.partial(combined_kernel, parts), out_shape=out_s...  126 us
    dot_general x1, matrix products, local(): upper = jnp.dot(normed_two, up_w, preferred_element_type=jnp.float32)  3.97 us
    dot_general x1, matrix products, attend(): jnp.dot(normed, qkv_w, preferred_element_type=jnp.float32)  2.91 us

profile of v15, /device:TPU:1, one launch (start us, length us, event | category | flops | bytes accessed | tf_op | source)
XLA Modules:
  0.0 139.3 jit_solution(17741613537410912964)
XLA Ops:
  0.6 0.0 copy-start
  0.7 0.7 fusion.20
  1.4 0.7 reduce.4
  2.1 59.9 %shard_map.85 = (bf16[8,4,64,384]{3,2,1,0:T(8,128)(2,1)}, bf16[64,512]{1,0:T(8,128)(2,1)}, bf16[2,4,2,24,2048]{4,3,2,1,0:T(8,128)(2,1)}) custom-call(f32[4,6144]{1,0:T(4,128)} %refs_0_.1, f32[4,8192]{1,0:T(4,128)} %refs_1_.1, bf16[24,2048]{1,0:T(8,128)(2,1)} %refs_2_.3), custom_call_target="tpu_custom_call" | custom-call | tf_op jit(solution)/shard_map/pallas_call | solution.py:379
  62.0 2.9 %convolution_convert_fusion.1 = bf16[384,384]{0,1:T(8,128)(2,1)S(1)} fusion(bf16[384,2048]{1,0:T(8,128)(2,1)} %bitcast.57, bf16[2048,384]{1,0:T(8,128)(2,1)} %bitcast.56), kind=kOutput, calls=%fused_computation.5 | convolution fusion | flops 604127232 | bytes 3440640 | tf_op jit(solution)/shard_map/dot_general | solution.py:392
  65.0 0.1 copy.15
  65.1 0.1 copy.14
  65.3 0.8 scatter_fusion
  66.2 0.0 copy-start.1
  66.2 0.4 fusion.25
  66.6 0.1 fusion.12
  66.7 0.0 copy-done
  66.7 2.0 %convolution_convert_fusion = bf16[384,2048]{1,0:T(8,128)(2,1)} fusion(bf16[128,2048]{1,0:T(8,128)(2,1)S(1)} %copy-done, f32[384,384]{0,1:T(8,128)S(1)} %get-tuple-element.24, f32[384]{0:T(512)S(1)} %fusion.12, f32[384]{0:T(512)S(1)} %get-tuple-element.23, bf16[384,1,3,128]{0,3,2,1:T(8,128)(2,1)S(1)} %bitcast.53), kind=kOutput, calls=%fused_computation.1 | convolution fusion | flops 240353280 | bytes 2789376 | tf_op jit(solution)/shard_map/dot_general | solution.py:459
  68.7 0.0 copy-done.1
  68.7 66.0 %shard_map.86 = (bf16[8,4,64,512]{3,2,1,0:T(8,128)(2,1)}, bf16[24,2048]{1,0:T(8,128)(2,1)}, bf16[2,4,2,24,2048]{4,3,2,1,0:T(8,128)(2,1)}) custom-call(bf16[64,512]{1,0:T(8,128)(2,1)} %get-tuple-element.9.refs_0_, bf16[2,4,2,24,2048]{4,3,2,1,0:T(8,128)(2,1)} %bitcast.48, bf16[24,2048]{1,0:T(8,128)(2,1)} %refs_2_.3), custom_call_target="tpu_custom_call" | custom-call | tf_op jit(solution)/shard_map/pallas_call | solution.py:379
  134.7 0.0 copy-start.2
  134.7 4.0 %fusion.10 = bf16[384,512]{1,0:T(8,128)(2,1)} fusion(bf16[384,2048]{1,0:T(8,128)(2,1)} %bitcast.55, bf16[2048,512]{1,0:T(8,128)(2,1)} %bitcast.54), kind=kOutput, calls=%fused_computation.16 | convolution fusion | flops 807075840 | bytes 4063232 | tf_op jit(solution)/shard_map/dot_general | solution.py:480
  138.7 0.0 copy-done.2
  138.7 0.6 copy.18
  (4 shorter events, 0.1 us)
Async XLA Ops:
  0.6 66.1 %copy-start = (bf16[128,2048]{1,0:T(8,128)(2,1)S(1)}, bf16[128,2048]{1,0:T(8,128)(2,1)}, u32[]{:S(2)}) copy-start(bf16[128,2048]{1,0:T(8,128)(2,1)} %param.11) | copy-start | bytes 1572868
  66.2 2.5 %copy-start.1 = (bf16[3,2,128,128]{3,2,1,0:T(8,128)(2,1)}, bf16[3,2,128,128]{3,2,1,0:T(8,128)(2,1)S(1)}, u32[]{:S(2)}) copy-start(bf16[3,2,128,128]{3,2,1,0:T(8,128)(2,1)S(1)} %scatter_fusion) | copy-start | bytes 589828
  134.7 4.0 %copy-start.2 = (bf16[24,2048]{1,0:T(8,128)(2,1)S(1)}, bf16[24,2048]{1,0:T(8,128)(2,1)}, u32[]{:S(2)}) copy-start(bf16[24,2048]{1,0:T(8,128)(2,1)} %get-tuple-element.28) | copy-start | bytes 294916
